TPU v7x, 32 devices: a whole 2x2x4 slice. The times are simulated.
32 devices in a mesh: occ: 4 (over y, core), aux: 8 (over z, x).
Axes of the slice: x: 2, y: 2, z: 4, core: 2. Of those that a mesh axis runs over, the one named last changes fastest.
Arguments:
- pair_ints: bfloat16 [16, 128, 20480], P(None, None, ('aux', 'occ')), may hold values from -110 to 110
- domain_len: int32 [4], replicated, may hold values from 1 to 4, as said below
- domain_blocks: int32 [4, 4], replicated, may hold values from 0 to 703
- slot_orbital: int32 [4], replicated, may hold values from 0 to 3, each once
- virt_energy: float32 [90112], replicated, may hold values from 0.1 to 3
- occ_energy: float32 [4], replicated, may hold values from -2 to -0.3
Outputs:
- projected: bfloat16 [4, 512, 20480], P('occ', None, 'aux')
Inputs may be any that keep to these rules, and one draw needn't show every extreme that they name: `domain_len`: some orbital has exactly 4 live blocks. `slot_orbital`: each orbital is owned by exactly one group.
All inputs are finite; a program needn't handle non-finite values.
Results may differ from a plain program's by a relative error of at most 0.001.
The roundings to bfloat16 on the way count: a program that leaves them out, or rounds other values in their place, can miss the bound.
Values may be sent and summed in bfloat16 or wider, within the bound.
A program may use at most 128 MiB of HBM per device.

v0:
```python
import jax
import jax.numpy as jnp
from jax import lax
from jax.sharding import PartitionSpec as P

LEVEL_RATIO = 0.5
EPSILON = 1e-05


def local(pair_ints, domain_len, domain_blocks, slot_orbital, virt_energy, occ_energy):
    orbitals = domain_len.shape[0]
    block_count = domain_blocks.shape[1]
    block_rows = pair_ints.shape[1]
    local_cols = pair_ints.shape[2]
    domain_size = block_count * block_rows
    slot_ids = jnp.arange(block_count, dtype=jnp.int32)
    ordered_len = jnp.take(domain_len, slot_orbital, axis=0)
    starts = (slot_orbital * block_count)[:, None] + slot_ids[None, :]
    live_mask = slot_ids[None, :] < ordered_len[:, None]
    flat_index = starts.reshape(-1)
    picked = jnp.take(pair_ints, flat_index, axis=0)
    picked = jnp.where(live_mask.reshape(-1)[:, None, None], picked, jnp.zeros_like(picked))
    padded = picked.reshape(orbitals, domain_size, local_cols)
    regrouped = lax.all_to_all(padded, "occ", split_axis=0, concat_axis=2, tiled=True)
    own_rows = regrouped[0]
    owner_group = lax.axis_index("occ")
    orbital = lax.dynamic_index_in_dim(slot_orbital, owner_group, 0, keepdims=False)
    partials = jnp.einsum("oac,obc->oab", padded, padded, preferred_element_type=jnp.float32)
    gram_part = lax.psum_scatter(
        partials.reshape(orbitals * domain_size, domain_size),
        ("occ", "aux"),
        scatter_dimension=0,
        tiled=True,
    )
    gram_sum = lax.all_gather(gram_part, "aux", axis=0, tiled=True)
    energy_table = virt_energy.reshape(-1, block_rows)
    blocks = lax.dynamic_index_in_dim(domain_blocks, orbital, 0, keepdims=False)
    energies = jnp.take(energy_table, blocks, axis=0).reshape(domain_size)
    occ_level = lax.dynamic_index_in_dim(occ_energy, orbital, 0, keepdims=False)
    denominator = energies[:, None] + energies[None, :] - 2.0 * occ_level
    amplitude = gram_sum / denominator
    length = lax.dynamic_index_in_dim(domain_len, orbital, 0, keepdims=False).astype(jnp.float32)
    level_shift = LEVEL_RATIO * (jnp.trace(amplitude) / (block_rows * length) + EPSILON)
    factor = jnp.linalg.cholesky(amplitude + level_shift * jnp.eye(domain_size, dtype=jnp.float32))
    solved = jax.scipy.linalg.cho_solve((factor, True), amplitude)
    projector = solved.T.astype(jnp.bfloat16)
    projected = jnp.dot(projector, own_rows, preferred_element_type=jnp.float32).astype(
        jnp.bfloat16
    )
    return projected[None]


def solution(mesh):
    placed = (P(None, None, ("aux", "occ")), P(), P(), P(), P(), P())
    return jax.shard_map(
        local, mesh=mesh, in_specs=placed, out_specs=P("occ", None, "aux"), check_vma=False
    )
```

profile of v0, /device:TPU:0, one launch (start us, length us, event | category | flops | bytes accessed | tf_op | source)
XLA Modules:
  0.0 391.1 jit_solution(3105162862275415704)
XLA Ops:
  9.7 2.4 gather_fusion.1
  14.2 3.8 fusion.62
  18.1 4.7 %all-to-all-start = ((bf16[4,512,640]{2,1,0:T(8,128)(2,1)}), bf16[4,512,640]{2,1,0:T(8,128)(2,1)}, u32[]{:S(2)}, u32[]{:S(2)}) async-start(bf16[4,512,640]{2,1,0:T(8,128)(2,1)} %copy-done.2), calls=%async_computation | async-start | bytes 5242880 | tf_op jit(solution)/shard_map/all_to_all | solution.py:24
  22.8 143.1 %reduce-scatter.4.cloned.1.call-done = f32[64,512]{1,0:T(8,128)} async-done(((f32[2048,512]{1,0:T(8,128)}), f32[64,512]{1,0:T(8,128)}) %reduce-scatter.4.cloned.1.call-update) | async-done | bytes 131088 | tf_op jit(solution)/shard_map/reduce_scatter | solution.py:29
  173.1 4.5 %copy.58 = bf16[1,512,4,640]{1,3,2,0:T(8,128)(2,1)} copy(bf16[1,512,4,640]{3,1,2,0:T(8,128)(2,1)} %bitcast.23) | data formatting | bytes 5242880 | tf_op jit(solution)/shard_map/all_to_all | solution.py:24
  177.7 28.7 %all-gather.2.cloned.1.call-done = f32[512,512]{1,0:T(8,128)} async-done(((f32[64,512]{1,0:T(8,128)}), f32[512,512]{1,0:T(8,128)}) %all-gather.2.cloned.1.call-update) | async-done | bytes 1048592 | tf_op jit(solution)/shard_map/all_gather | solution.py:35
  206.4 2.6 copy.45
  209.0 3.2 select_reduce_fusion
  212.9 2.3 select_add_fusion
  215.2 2.5 copy.46
  220.5 11.7 %cholesky.103 = f32[128,128]{1,0:T(8,128)S(1)} custom-call(f32[128,128]{1,0:T(8,128)S(1)} %cholesky.263), custom_call_target="Cholesky" | custom-call | tf_op jit(solution)/shard_map/jit(cholesky)/cholesky | solution.py:44
  232.3 9.8 %custom-call.34 = f32[1,128,128]{1,2,0:T(8,128)S(1)} custom-call(f32[1,128,128]{2,1,0:T(8,128)S(1)} %get-tuple-element.46), custom_call_target="InvertDiagBlocksLowerTriangular" | custom-call | tf_op jit(solution)/shard_map/jit(cholesky)/cholesky | solution.py:44
  244.6 11.7 %cholesky.215 = f32[128,128]{1,0:T(8,128)S(1)} custom-call(f32[128,128]{1,0:T(8,128)S(1)} %cholesky.267), custom_call_target="Cholesky" | custom-call | tf_op jit(solution)/shard_map/jit(cholesky)/cholesky | solution.py:44
  256.7 10.0 %custom-call.35 = f32[1,128,128]{1,2,0:T(8,128)S(1)} custom-call(f32[1,128,128]{2,1,0:T(8,128)S(1)} %get-tuple-element.44), custom_call_target="InvertDiagBlocksLowerTriangular" | custom-call | tf_op jit(solution)/shard_map/jit(cholesky)/cholesky | solution.py:44
  269.7 11.7 %cholesky.236 = f32[128,128]{1,0:T(8,128)S(1)} custom-call(f32[128,128]{1,0:T(8,128)S(1)} %cholesky.272), custom_call_target="Cholesky" | custom-call | tf_op jit(solution)/shard_map/jit(cholesky)/cholesky | solution.py:44
  282.2 9.8 %custom-call.36 = f32[1,128,128]{1,2,0:T(8,128)S(1)} custom-call(f32[1,128,128]{2,1,0:T(8,128)S(1)} %get-tuple-element.42), custom_call_target="InvertDiagBlocksLowerTriangular" | custom-call | tf_op jit(solution)/shard_map/jit(cholesky)/cholesky | solution.py:44
  294.5 12.1 %cholesky.253 = f32[128,128]{1,0:T(8,128)S(1)} custom-call(f32[128,128]{1,0:T(8,128)S(1)} %convolution_subtract_fusion.8), custom_call_target="Cholesky" | custom-call | tf_op jit(solution)/shard_map/jit(cholesky)/cholesky | solution.py:44
  312.6 2.4 select_select_fusion
  315.0 14.2 %while.1 = (s32[]{:T(128)}, f32[512,512]{0,1:T(8,128)}, s32[4,2]{0,1:T(2,128)S(1)}, f32[4,128,128]{2,1,0:T(8,128)}, s32[]{:T(128)}) while((s32[]{:T(128)}, f32[512,512]{0,1:T(8,128)}, s32[4,2]{0,1:T(2,128)S(1)}, f32[4,128,128]{2,1,0:T(8,128)}, s32[]{:T(128)}) %tuple.32), condition=%wide.while_cond, body=%wide.while_body.sunk | while | flops 2 | bytes 393829 | solution.py:45
  315.6 2.2 dynamic-slice.7
  319.2 2.2 dynamic-slice.7
  329.2 40.1 %custom-call.37 = f32[4,128,128]{1,2,0:T(8,128)S(1)} custom-call(f32[4,128,128]{2,1,0:T(8,128)} %get-tuple-element.12), custom_call_target="InvertDiagBlocksLowerTriangular" | custom-call | tf_op jit(solution)/shard_map/jit(_cho_solve)/triangular_solve | solution.py:45
  375.3 2.4 convolution_subtract_fusion.5
  381.1 3.1 fusion
  (109 shorter events, 43.3 us)
Async XLA Ops:
  6.5 3.2 copy-start
  6.5 159.4 %reduce-scatter.4.cloned.1.call-start = ((), (), s32[]{:S(2)}) async-start(), calls=%async_computation.3 | async-start | bytes 4325376 | tf_op jit(solution)/shard_map/reduce_scatter | solution.py:29
  14.2 3.8 copy-start.2
  18.0 147.9 %copy-start.7 = (s32[4]{0:T(128)S(1)}, s32[4]{0:T(128)}, u32[]{:S(2)}) copy-start(s32[4]{0:T(128)} %param.9) | copy-start | bytes 52
  18.0 150.7 %copy-start.1 = (s32[4]{0:T(128)S(1)}, s32[4]{0:T(128)}, u32[]{:S(2)}) copy-start(s32[4]{0:T(128)} %param.7) | copy-start | bytes 52
  18.0 151.3 %copy-start.9 = (f32[4]{0:T(128)S(1)}, f32[4]{0:T(128)}, u32[]{:S(2)}) copy-start(f32[4]{0:T(128)} %param.11) | copy-start | bytes 52
  18.0 152.7 %copy-start.8 = (s32[4,4]{1,0:T(4,128)S(1)}, s32[4,4]{1,0:T(4,128)}, u32[]{:S(2)}) copy-start(s32[4,4]{1,0:T(4,128)} %param.8) | copy-start | bytes 196
  18.1 155.1 %all-to-all-start = ((bf16[4,512,640]{2,1,0:T(8,128)(2,1)}), bf16[4,512,640]{2,1,0:T(8,128)(2,1)}, u32[]{:S(2)}, u32[]{:S(2)}) async-start(bf16[4,512,640]{2,1,0:T(8,128)(2,1)} %copy-done.2), calls=%async_computation | async-start | bytes 5242880 | tf_op jit(solution)/shard_map/all_to_all | solution.py:24
  22.8 183.7 %all-gather.2.cloned.1.call-start = ((), (), s32[]{:S(2)}) async-start(), calls=%async_computation.2 | async-start | bytes 1179648 | tf_op jit(solution)/shard_map/all_gather | solution.py:35
  219.5 1.0 copy-start.5
  267.2 1.0 copy-start.3
  369.3 5.9 %copy-start.4 = (f32[512,512]{0,1:T(8,128)S(1)}, f32[512,512]{0,1:T(8,128)}, u32[]{:S(2)}) copy-start(f32[512,512]{0,1:T(8,128)} %get-tuple-element.107) | copy-start | bytes 3145732
  378.5 2.6 copy-start.6
Sparse Core Ops, SparseCore 0:
  18.1 147.7 reduce-scatter.3
  168.0 38.3 all-gather.1
where the time goes:
time: 395 us; the launch traced here: 391 us
  waiting for transfers between devices  172 us (44%)
  other arithmetic  133 us (34%)
  local copies, waits for them, and re-layouts  35.3 us (9%)
  matrix products  25.2 us (6%)
  between operations  20.7 us (5%)
  starting transfers between devices  4.74 us (1%)
    reduce_scatter x1, waiting for transfers between devices, local(): lax.psum_scatter(partials.reshape(orbitals * domain_size, domain_size), (...  143 us
    another operation x15, other arithmetic, local(): jnp.linalg.cholesky(amplitude + level_shift * jnp.eye(domain_size, dtype=...  79.7 us
    another operation x3, other arithmetic, local(): solved = jax.scipy.linalg.cho_solve((factor, True), amplitude)  42.5 us
    all_gather x1, waiting for transfers between devices, local(): gram_sum = lax.all_gather(gram_part, 'aux', axis=0, tiled=True)  28.7 us
    another operation x20, local copies, waits for them, and re-layouts  14.2 us
    another operation x14, matrix products, local(): solved = jax.scipy.linalg.cho_solve((factor, True), amplitude)  11.6 us
  transfers between devices with their start and end apart: 3, of which 2 were waited for; matrix products, arithmetic and copies ran while one was open for 2% of the time, Pallas kernels for 0%

commit v1 on v0

v1 whole, which is shorter than its diff:
```python
import jax
import jax.numpy as jnp
from jax import lax
from jax.experimental import pallas as pl
from jax.experimental.pallas import tpu as pltpu
from jax.sharding import PartitionSpec as P

LEVEL_RATIO = 0.5
EPSILON = 1e-05
F32 = jnp.float32
BF16 = jnp.bfloat16


def split(value):
    high = value.astype(BF16)
    return high, (value - high.astype(F32)).astype(BF16)


def dot(a, b):
    return jnp.dot(a, b, preferred_element_type=F32)


def solve_kernel(
    scale_ref, gram_ref, col_ref, row_ref, rows_hbm, out_hbm,
    m_high, m_low, x_ref, r_ref, rows_buf, out_buf, in_sem, out_sem,
):
    size = gram_ref.shape[0]
    tiles, _, width = out_buf.shape

    def fetch(t):
        return pltpu.make_async_copy(
            rows_hbm.at[:, pl.ds(t * width, width)], rows_buf.at[t], in_sem.at[t]
        )

    def flush(t):
        return pltpu.make_async_copy(
            out_buf.at[t], out_hbm.at[:, pl.ds(t * width, width)], out_sem.at[t]
        )

    for t in range(tiles):
        fetch(t).start()

    eye = (
        lax.broadcasted_iota(jnp.int32, (size, size), 0)
        == lax.broadcasted_iota(jnp.int32, (size, size), 1)
    ).astype(F32)
    amplitude = gram_ref[...] / (col_ref[...] + row_ref[...] - 2.0 * scale_ref[0])
    trace = jnp.sum(amplitude * eye)
    level_shift = LEVEL_RATIO * (trace / scale_ref[1] + EPSILON)
    row_sum = jnp.max(jnp.sum(jnp.abs(amplitude), axis=0, keepdims=True))
    upper = level_shift + 1.01 * jnp.minimum(row_sum, 1.01 * trace)
    unit = 2.0 / (level_shift + upper)
    start = level_shift * unit
    scaled = (amplitude + level_shift * eye) * unit
    high, low = split(scaled)
    m_high[...] = high
    m_low[...] = low

    def factor(rho):
        return 2.0 / (1.0 + rho * (2.0 - rho))

    def advance(rho):
        return factor(rho) * rho * (2.0 - rho)

    x_ref[...] = factor(start) * (2.0 * eye - scaled)

    def quick(rho):
        x = x_ref[...]
        xb = x.astype(BF16)
        t = dot(m_high[...], xb)
        x_ref[...] = factor(rho) * (2.0 * x - dot(xb, t.astype(BF16)))
        return advance(rho)

    rho = lax.while_loop(lambda rho: rho < 0.95, quick, advance(start))
    del rho

    def times_m(x):
        xh, xl = split(x)
        mh = m_high[...]
        return dot(mh, xh) + (dot(mh, xl) + dot(m_low[...], xh))

    def residual():
        r = eye_again() - times_m(x_ref[...])
        r_ref[...] = r
        return jnp.sum(r * r)

    def eye_again():
        return (
            lax.broadcasted_iota(jnp.int32, (size, size), 0)
            == lax.broadcasted_iota(jnp.int32, (size, size), 1)
        ).astype(F32)

    def x_times(value):
        xh, xl = split(x_ref[...])
        vh, vl = split(value)
        return dot(xh, vh) + (dot(xh, vl) + dot(xl, vh))

    norm = residual()

    def careful(rho):
        x_ref[...] = factor(rho) * (2.0 * x_ref[...] - x_times(times_m(x_ref[...])))
        return advance(rho)

    def restart(_):
        x_ref[...] = eye_again()
        lax.while_loop(lambda rho: rho < 0.9999, careful, start)
        return residual()

    norm = lax.cond(norm < 0.9, lambda n: n, restart, norm)

    def refine(state):
        _, step = state
        x_ref[...] = x_ref[...] + x_times(r_ref[...])
        return residual(), step + 1

    lax.while_loop(
        lambda state: jnp.logical_and(state[0] > 1e-6, state[1] < 12), refine, (norm, 0)
    )
    x = x_ref[...] + x_times(r_ref[...])
    projector = (eye_again() - (level_shift * unit) * x).astype(BF16)
    m_high[...] = projector
    for t in range(tiles):
        fetch(t).wait()
        out_buf[t] = dot(m_high[...], rows_buf[t]).astype(BF16)
        flush(t).start()
    for t in range(tiles):
        flush(t).wait()


def solve_and_project(scales, gram, energies, rows):
    size, cols = rows.shape
    tiles = max(1, cols // 512)
    while cols % tiles or (cols // tiles) % 128:
        tiles -= 1
    width = cols // tiles
    vmem = pl.BlockSpec(memory_space=pltpu.VMEM)
    return pl.pallas_call(
        solve_kernel,
        out_shape=jax.ShapeDtypeStruct((size, cols), BF16),
        in_specs=[
            pl.BlockSpec(memory_space=pltpu.SMEM), vmem, vmem, vmem,
            pl.BlockSpec(memory_space=pl.ANY),
        ],
        out_specs=pl.BlockSpec(memory_space=pl.ANY),
        scratch_shapes=[
            pltpu.VMEM((size, size), BF16),
            pltpu.VMEM((size, size), BF16),
            pltpu.VMEM((size, size), F32),
            pltpu.VMEM((size, size), F32),
            pltpu.VMEM((tiles, size, width), BF16),
            pltpu.VMEM((tiles, size, width), BF16),
            pltpu.SemaphoreType.DMA((tiles,)),
            pltpu.SemaphoreType.DMA((tiles,)),
        ],
        compiler_params=pltpu.CompilerParams(vmem_limit_bytes=48 << 20),
        name="solve",
    )(scales, gram, energies[:, None], energies[None, :], rows)


def local(pair_ints, domain_len, domain_blocks, slot_orbital, virt_energy, occ_energy):
    orbitals = domain_len.shape[0]
    block_count = domain_blocks.shape[1]
    block_rows = pair_ints.shape[1]
    local_cols = pair_ints.shape[2]
    domain_size = block_count * block_rows
    slot_ids = jnp.arange(block_count, dtype=jnp.int32)
    ordered_len = jnp.take(domain_len, slot_orbital, axis=0)
    starts = (slot_orbital * block_count)[:, None] + slot_ids[None, :]
    live_mask = slot_ids[None, :] < ordered_len[:, None]
    picked = jnp.take(pair_ints, starts.reshape(-1), axis=0)
    picked = jnp.where(live_mask.reshape(-1)[:, None, None], picked, jnp.zeros_like(picked))
    padded = picked.reshape(orbitals, domain_size, local_cols)
    own_rows = lax.all_to_all(padded, "occ", split_axis=0, concat_axis=2, tiled=True)[0]
    orbital = lax.dynamic_index_in_dim(slot_orbital, lax.axis_index("occ"), 0, keepdims=False)
    gram = lax.psum(jnp.einsum("ac,bc->ab", own_rows, own_rows, preferred_element_type=F32), "aux")
    blocks = lax.dynamic_index_in_dim(domain_blocks, orbital, 0, keepdims=False)
    energies = jnp.take(virt_energy.reshape(-1, block_rows), blocks, axis=0).reshape(domain_size)
    occ_level = lax.dynamic_index_in_dim(occ_energy, orbital, 0, keepdims=False)
    length = lax.dynamic_index_in_dim(domain_len, orbital, 0, keepdims=False).astype(F32)
    scales = jnp.stack([occ_level, block_rows * length])
    return solve_and_project(scales, gram, energies, own_rows)[None]


def solution(mesh):
    placed = (P(None, None, ("aux", "occ")), P(), P(), P(), P(), P())
    return jax.shard_map(
        local, mesh=mesh, in_specs=placed, out_specs=P("occ", None, "aux"), check_vma=False
    )
```

time: 395 us -> 157 us (0.40)
  other arithmetic: 133 us -> 4.58 us
  waiting for transfers between devices: 172 us -> 65.8 us
  blocking collectives: 0 us -> 35.4 us
  matrix products: 25.2 us -> 2.57 us
  local copies, waits for them, and re-layouts: 35.3 us -> 17.7 us
  Pallas kernels: 0 us -> 14.5 us
  starting transfers between devices: 4.74 us -> 0.01 us
  between operations: 20.7 us -> 16.2 us
    reduce_scatter x1 -> x0, waiting for transfers between devices: 143 us -> none  [local(): lax.psum_scatter(partials.reshape(orbitals * domain_size, domain_size), (...]
    another operation x18 -> x1, other arithmetic: 122 us -> 0.75 us  [local(): scales = jnp.stack([occ_level, block_rows * length])]
    psum x0 -> x1, waiting for transfers between devices: none -> 65.8 us  [local(): lax.psum(jnp.einsum('ac,bc->ab', own_rows, own_rows, preferred_element_ty...]
    all_to_all x0 -> x1, blocking collectives: none -> 35.4 us  [local(): lax.all_to_all(padded, 'occ', split_axis=0, concat_axis=2, tiled=True)[0]]
    all_gather x1 -> x0, waiting for transfers between devices: 28.7 us -> none  [local(): gram_sum = lax.all_gather(gram_part, 'aux', axis=0, tiled=True)]
    another operation x20 -> x0, matrix products: 18.4 us -> none  [the longest x14 11.6 us: local(): solved = jax.scipy.linalg.cho_solve((factor, True), amplitude)]
    another operation x34 -> x0, local copies, waits for them, and re-layouts: 16.1 us -> none
    pallas_call x0 -> x1, Pallas kernels: none -> 14.5 us  [solve_and_project(): pl.pallas_call(solve_kernel, out_shape=jax.ShapeDtypeStruct((size, cols),...]
  transfers between devices with their start and end apart: 3 -> 1, of which waited for: 2 -> 1; matrix products, arithmetic and copies ran while one was open for 2% -> 6% of each run, Pallas kernels for 0% -> 0%
where the time goes in v1:
time: 157 us
  waiting for transfers between devices  65.8 us (42%)
  blocking collectives  35.4 us (23%)
  local copies, waits for them, and re-layouts  17.7 us (11%)
  between operations  16.2 us (10%)
  Pallas kernels  14.5 us (9%)
  other arithmetic  4.58 us (3%)
  matrix products  2.57 us (2%)
    psum x1, waiting for transfers between devices, local(): lax.psum(jnp.einsum('ac,bc->ab', own_rows, own_rows, preferred_element_ty...  65.8 us
    all_to_all x1, blocking collectives, local(): lax.all_to_all(padded, 'occ', split_axis=0, concat_axis=2, tiled=True)[0]  35.4 us
    pallas_call x1, Pallas kernels, solve_and_project(): pl.pallas_call(solve_kernel, out_shape=jax.ShapeDtypeStruct((size, cols),...  14.5 us
    unnamed x21, local copies, waits for them, and re-layouts  6.56 us
    all_to_all x1, local copies, waits for them, and re-layouts, local(): lax.all_to_all(padded, 'occ', split_axis=0, concat_axis=2, tiled=True)[0]  3.76 us
  transfers between devices with their start and end apart: 1, of which 1 were waited for; matrix products, arithmetic and copies ran while one was open for 6% of the time, Pallas kernels for 0%

profile of v1, /device:TPU:0, one launch (start us, length us, event | category | flops | bytes accessed | tf_op | source)
XLA Modules:
  0.0 156.7 jit_solution(2404120576689051022)
XLA Ops:
  6.5 0.8 compare_select_fusion.4
  7.4 1.3 gather_fusion
  8.6 0.7 and_select_fusion
  9.4 0.1 iota_compare_fusion
  9.5 0.1 broadcast_bitcast_fusion.1
  9.5 0.1 add.79
  9.6 0.1 broadcast_bitcast_fusion
  9.7 2.4 %gather_fusion.1 = bf16[16,128,640]{2,1,0:T(8,128)(2,1)} fusion(bf16[16,128,640]{2,1,0:T(8,128)(2,1)S(1)} %copy-done, s32[1024]{0:T(1024)S(1)} %pad_clamp_fusion.1), kind=kCustom, calls=%fused_computation.1 | custom fusion | bytes 5242944 | tf_op jit(solution)/shard_map/jit(_take)/gather | solution.py:170
  12.1 2.1 %fusion.2 = bf16[4,512,640]{2,1,0:T(8,128)(2,1)S(1)} fusion(pred[4,512]{1,0:T(4,128)(4,1)S(1)} %bitcast.49, pred[4,512]{1,0:T(4,128)(4,1)S(1)} %bitcast.48, bf16[4,512,640]{2,1,0:T(8,128)(2,1)} %bitcast.47), kind=kLoop, calls=%fused_computation.6 | loop fusion | flops 2621440 | bytes 5246976 | tf_op jit(solution)/shard_map/jit(_where)/select_n | solution.py:171
  14.2 35.4 %all_to_all.15 = bf16[4,512,640]{2,1,0:T(8,128)(2,1)S(1)} all-to-all(bf16[4,512,640]{2,1,0:T(8,128)(2,1)S(1)} %fusion.2), channel_id=1, replica_groups=mesh['occ'=4,'aux'=8] {'occ'}, dimensions={0} | all-to-all | bytes 5242880 | tf_op jit(solution)/shard_map/all_to_all | solution.py:173
  49.6 1.5 copy-done.4
  51.1 2.6 %fusion.3 = f32[512,512]{1,0:T(8,128)} fusion(bf16[4,512,640]{2,1,0:T(8,128)(2,1)S(1)} %all_to_all.15), kind=kOutput, calls=%fused_computation.7 | convolution fusion | flops 1342177280 | bytes 3670016 | tf_op jit(solution)/shard_map/ac,bc->ab/dot_general | solution.py:175
  53.7 0.7 dynamic_slice.15
  56.4 0.7 dynamic_slice.17
  57.7 0.7 dynamic_slice.16
  58.4 1.6 gather_fusion.2
  60.0 0.1 copy.9.col_ref
  60.2 0.7 pad_maximum_fusion.scale_ref
  60.9 3.8 %copy.8 = bf16[1,512,4,640]{3,2,1,0:T(4,128)(2,1)S(1)} copy(bf16[1,512,4,640]{3,1,2,0:T(8,128)(2,1)} %bitcast.45) | data formatting | bytes 5242880 | tf_op jit(solution)/shard_map/all_to_all | solution.py:173
  64.7 1.9 %copy.12 = bf16[64,8,4,640]{3,1,2,0:T(8,128)(2,1)} copy(bf16[64,8,4,640]{3,2,1,0:T(4,128)(2,1)S(1)} %bitcast.46) | data formatting | bytes 5242880
  66.6 65.8 %all-reduce.2.cloned.1.call-done.gram_ref = f32[512,512]{1,0:T(8,128)} async-done(((f32[512,512]{1,0:T(8,128)}), f32[512,512]{1,0:T(8,128)}) %all-reduce.2.cloned.1.call-update) | async-done | bytes 1048592 | tf_op jit(solution)/shard_map/psum | solution.py:175
  132.4 1.7 %copy-done.1 = bf16[64,8,4,640]{3,1,2,0:T(8,128)(2,1)S(1)} copy-done((bf16[64,8,4,640]{3,1,2,0:T(8,128)(2,1)S(1)}, bf16[64,8,4,640]{3,1,2,0:T(8,128)(2,1)}, u32[]{:S(2)}) %copy-start.1) | copy-done | bytes 2621464
  134.1 1.2 copy-done.2
  135.3 14.5 %solve.1 = bf16[512,2560]{1,0:T(8,128)(2,1)} custom-call(f32[2]{0:T(128)S(1)} %pad_maximum_fusion.scale_ref, f32[512,512]{1,0:T(8,128)S(1)} %copy-done.2, f32[512,1]{1,0:T(8,128)S(1)} %copy.9.col_ref, f32[1,512]{1,0:T(1,128)S(1)} %bitcast.44, bf16[512,2560]{1,0:T(8,128)(2,1)S(1)} %bitcast.42), custom_call_target="tpu_custom_call" | custom-call | tf_op jit(solution)/shard_map/solve/pallas_call | solution.py:137
  (25 shorter events, 0.3 us)
Async XLA Ops:
  6.5 3.2 %copy-start = (bf16[16,128,640]{2,1,0:T(8,128)(2,1)S(1)}, bf16[16,128,640]{2,1,0:T(8,128)(2,1)}, u32[]{:S(2)}) copy-start(bf16[16,128,640]{2,1,0:T(8,128)(2,1)} %param.6) | copy-start | bytes 7864324
  6.5 125.8 %all-reduce.2.cloned.1.call-start = ((), (), s32[]{:S(2)}) async-start(), calls=%async_computation.1 | async-start | bytes 2097152 | tf_op jit(solution)/shard_map/psum | solution.py:175
  49.6 1.5 copy-start.4
  51.1 2.6 %copy-start.5 = (s32[4]{0:T(128)S(1)}, s32[4]{0:T(128)}, u32[]{:S(2)}) copy-start(s32[4]{0:T(128)} %param.9) | copy-start | bytes 52
  51.1 5.3 %copy-start.3 = (s32[4]{0:T(128)S(1)}, s32[4]{0:T(128)}, u32[]{:S(2)}) copy-start(s32[4]{0:T(128)} %param.7) | copy-start | bytes 52
  51.1 6.6 %copy-start.7 = (f32[4]{0:T(128)S(1)}, f32[4]{0:T(128)}, u32[]{:S(2)}) copy-start(f32[4]{0:T(128)} %param.11) | copy-start | bytes 52
  51.1 7.3 %copy-start.6 = (s32[4,4]{1,0:T(4,128)S(1)}, s32[4,4]{1,0:T(4,128)}, u32[]{:S(2)}) copy-start(s32[4,4]{1,0:T(4,128)} %param.8) | copy-start | bytes 196
  132.4 1.7 %copy-start.1 = (bf16[64,8,4,640]{3,1,2,0:T(8,128)(2,1)S(1)}, bf16[64,8,4,640]{3,1,2,0:T(8,128)(2,1)}, u32[]{:S(2)}) copy-start(bf16[64,8,4,640]{3,1,2,0:T(8,128)(2,1)} %copy.12) | copy-start | bytes 7864324
  134.1 1.2 copy-start.2
Sparse Core Ops, SparseCore 0:
  53.8 78.5 all-reduce.1

commit v2 on v1

v2 whole, which is shorter than its diff:
```python
import functools

import jax
import jax.numpy as jnp
from jax import lax
from jax.experimental import pallas as pl
from jax.experimental.pallas import tpu as pltpu
from jax.sharding import PartitionSpec as P

LEVEL_RATIO = 0.5
EPSILON = 1e-05
F32 = jnp.float32
BF16 = jnp.bfloat16


def split(value):
    high = value.astype(BF16)
    return high, (value - high.astype(F32)).astype(BF16)


def dot(a, b):
    return jnp.dot(a, b, preferred_element_type=F32)


def gather_kernel(slot_ref, len_ref, pair_ref, padded_ref, packed_ref):
    blocks, size, cols = pair_ref.shape
    length = len_ref[slot_ref[pl.program_id(0)]]
    for k in range(blocks):
        rows = pair_ref[k]
        padded_ref[0, k * size:(k + 1) * size, :] = jnp.where(k < length, rows, jnp.zeros_like(rows))
    place = 0
    for i in range(blocks):
        band = lax.dot_general(
            padded_ref[0, i * size:(i + 1) * size, :],
            padded_ref[0, :(i + 1) * size, :],
            (((1,), (1,)), ((), ())),
            preferred_element_type=F32,
        )
        for j in range(i + 1):
            packed_ref[0, place * size:(place + 1) * size, :] = band[:, j * size:(j + 1) * size]
            place += 1


def gather_and_gram(slot_orbital, domain_len, pair_ints, blocks):
    groups = slot_orbital.shape[0]
    _, size, cols = pair_ints.shape
    packed = blocks * (blocks + 1) // 2 * size
    return pl.pallas_call(
        gather_kernel,
        out_shape=(
            jax.ShapeDtypeStruct((groups, blocks * size, cols), BF16),
            jax.ShapeDtypeStruct((groups, packed, size), F32),
        ),
        grid_spec=pltpu.PrefetchScalarGridSpec(
            num_scalar_prefetch=2,
            grid=(groups,),
            in_specs=[pl.BlockSpec((blocks, size, cols), lambda g, slot, _: (slot[g], 0, 0))],
            out_specs=[
                pl.BlockSpec((1, blocks * size, cols), lambda g, *_: (g, 0, 0)),
                pl.BlockSpec((1, packed, size), lambda g, *_: (g, 0, 0)),
            ],
        ),
        compiler_params=pltpu.CompilerParams(dimension_semantics=("arbitrary",)),
        name="gather",
    )(slot_orbital, domain_len, pair_ints)


MESH = pl.DeviceIdType.MESH


def exchange_kernel(
    ny, nx, nz, part_ref, rows_ref, gram_ref, own_ref,
    core_buf, y_out, y_in, x_out, x_in, z_out, z_in,
    core_ss, core_rs, y_ss, y_rs, x_ss, x_rs, z_ss, z_rs,
    gz_ss, gz_rs, gx_ss, gx_rs, row_ss, row_rs,
):
    occ, aux = lax.axis_index("occ"), lax.axis_index("aux")
    y, core = lax.div(occ, 2), lax.rem(occ, 2)
    z, x = lax.div(aux, nx), lax.rem(aux, nx)
    piece = gram_ref.shape[0] // (nx * nz)
    chunk = piece * nz
    other = 1 - core

    def at_y(d):
        return lax.rem(y + d, ny)

    def at_x(e):
        return lax.rem(x + e, nx)

    def at_z(f):
        return lax.rem(z + f, nz)

    def chunk_of(e):
        return pl.ds(pl.multiple_of(at_x(e) * chunk, 8), chunk)

    def piece_of(xx, zz):
        return pl.ds(pl.multiple_of((xx * nz + zz) * piece, 8), piece)

    def copy(src, dst, ss, rs, to_occ, to_aux):
        return pltpu.make_async_remote_copy(
            src_ref=src, dst_ref=dst, send_sem=ss, recv_sem=rs,
            device_id=(to_occ, to_aux), device_id_type=MESH,
        )

    barrier = pltpu.get_barrier_semaphore()
    peers = [(2 * y + other, aux)]
    for d in range(1, ny):
        peers += [(2 * at_y(d) + core, aux), (2 * at_y(d) + other, aux)]
    peers += [(occ, z * nx + at_x(e)) for e in range(1, nx)]
    peers += [(occ, at_z(f) * nx + x) for f in range(1, nz)]
    for peer in peers:
        pl.semaphore_signal(barrier, inc=1, device_id=peer, device_id_type=MESH)
    pl.semaphore_wait(barrier, len(peers))

    far_y = list(range(1, ny)) + [0]
    far_x = list(range(1, nx)) + [0]
    far_z = list(range(1, nz)) + [0]

    def core_copy(d, e):
        return copy(
            part_ref.at[2 * at_y(d) + other, chunk_of(e)], core_buf.at[d, chunk_of(e)],
            core_ss.at[d, e], core_rs.at[d, e], 2 * y + other, aux,
        )

    def y_copy(d, e):
        return copy(
            y_out.at[d, chunk_of(e)], y_in.at[d, chunk_of(e)],
            y_ss.at[d, e], y_rs.at[d, e], 2 * at_y(d) + core, aux,
        )

    def x_copy(e, f):
        return copy(
            x_out.at[piece_of(at_x(e), at_z(f))], x_in.at[e, pl.ds(pl.multiple_of(at_z(f) * piece, 8), piece)],
            x_ss.at[e, f], x_rs.at[e, f], occ, z * nx + at_x(e),
        )

    def z_copy(f):
        return copy(
            z_out.at[f], z_in.at[f], z_ss.at[f], z_rs.at[f], occ, at_z(f) * nx + x,
        )

    def gz_copy(f):
        mine = gram_ref.at[piece_of(x, z)]
        return copy(mine, mine, gz_ss.at[f], gz_rs.at[f], occ, at_z(f) * nx + x)

    def gz_in(f):
        theirs = gram_ref.at[piece_of(x, lax.rem(z + nz - f, nz))]
        return copy(theirs, theirs, gz_ss.at[f], gz_rs.at[f], occ, at_z(f) * nx + x)

    def gx_copy(e, f):
        part = gram_ref.at[piece_of(x, lax.rem(z + nz - f, nz))]
        return copy(part, part, gx_ss.at[e, f], gx_rs.at[e, f], occ, z * nx + at_x(e))

    def gx_in(e, f):
        part = gram_ref.at[piece_of(lax.rem(x + nx - e, nx), lax.rem(z + nz - f, nz))]
        return copy(part, part, gx_ss.at[e, f], gx_rs.at[e, f], occ, z * nx + at_x(e))

    def row_copy(d, swap):
        target = 2 * at_y(d) + (other if swap else core)
        return copy(
            rows_ref.at[target], own_ref.at[occ], row_ss.at[d, swap], row_rs.at[d, swap], target, aux
        )

    def row_in(d, swap):
        source = 2 * lax.rem(y + ny - d, ny) + (other if swap else core)
        return copy(
            rows_ref.at[source], own_ref.at[source], row_ss.at[d, swap], row_rs.at[d, swap], source, aux
        )

    row_moves = [(d, s) for d in range(1, ny) for s in (0, 1)] + [(0, 1)]

    for d in far_y:
        for e in far_x:
            core_copy(d, e).start()
    for e in far_x:
        for d in range(1, ny):
            core_copy(d, e).wait_recv()
            y_out[d, chunk_of(e), :] = part_ref[2 * at_y(d) + core, chunk_of(e), :] + core_buf[d, chunk_of(e), :]
            y_copy(d, e).start()
    for move in row_moves:
        row_copy(*move).start()
    for e in far_x:
        core_copy(0, e).wait_recv()
        for d in range(1, ny):
            y_copy(d, e).wait_recv()
        for f in far_z:
            if e:
                span = piece_of(at_x(e), at_z(f))
                total = part_ref[occ, span, :] + core_buf[0, span, :]
                for d in range(1, ny):
                    total = total + y_in[d, span, :]
                x_out[span, :] = total
                x_copy(e, f).start()
    for f in far_z:
        span = piece_of(x, at_z(f))
        total = part_ref[occ, span, :] + core_buf[0, span, :]
        for d in range(1, ny):
            total = total + y_in[d, span, :]
        for e in range(1, nx):
            x_copy(e, f).wait_recv()
            total = total + x_in[e, pl.ds(pl.multiple_of(at_z(f) * piece, 8), piece), :]
        if f:
            z_out[f] = total
            z_copy(f).start()
        else:
            z_out[0] = total
    total = z_out[0]
    for f in range(1, nz):
        z_copy(f).wait_recv()
        total = total + z_in[f]
    gram_ref[piece_of(x, z), :] = total
    for f in range(1, nz):
        gz_copy(f).start()
    for e in range(1, nx):
        gx_copy(e, 0).start()
    for f in range(1, nz):
        gz_in(f).wait_recv()
        for e in range(1, nx):
            gx_copy(e, f).start()
    for e in range(1, nx):
        for f in range(nz):
            gx_in(e, f).wait_recv()
    for move in row_moves:
        row_in(*move).wait_recv()

    for d in far_y:
        for e in far_x:
            core_copy(d, e).wait_send()
            if d:
                y_copy(d, e).wait_send()
    for f in far_z:
        for e in range(1, nx):
            x_copy(e, f).wait_send()
            gx_copy(e, f).wait_send()
        if f:
            z_copy(f).wait_send()
            gz_copy(f).wait_send()
    for move in row_moves:
        row_copy(*move).wait_send()


def exchange(packed, padded, n_aux):
    groups, height, lanes = packed.shape
    ny = groups // 2
    nx = ny if n_aux % ny == 0 else 1
    nz = n_aux // nx
    piece = height // n_aux
    dma = pltpu.SemaphoreType.DMA
    sems = [(ny, nx)] * 4 + [(nx, nz)] * 2 + [(nz,)] * 4 + [(nx, nz)] * 2 + [(ny, 2)] * 2
    return pl.pallas_call(
        functools.partial(exchange_kernel, ny, nx, nz),
        out_shape=(
            jax.ShapeDtypeStruct((height, lanes), F32),
            jax.ShapeDtypeStruct(padded.shape, BF16),
        ),
        in_specs=[pl.BlockSpec(memory_space=pltpu.VMEM), pl.BlockSpec(memory_space=pl.ANY)],
        out_specs=[pl.BlockSpec(memory_space=pltpu.VMEM), pl.BlockSpec(memory_space=pl.ANY)],
        scratch_shapes=[
            pltpu.VMEM((ny, height, lanes), F32),
            pltpu.VMEM((ny, height, lanes), F32),
            pltpu.VMEM((ny, height, lanes), F32),
            pltpu.VMEM((height, lanes), F32),
            pltpu.VMEM((nx, piece * nz, lanes), F32),
            pltpu.VMEM((nz, piece, lanes), F32),
            pltpu.VMEM((nz, piece, lanes), F32),
        ] + [dma(shape) for shape in sems],
        compiler_params=pltpu.CompilerParams(
            collective_id=0, has_side_effects=True, vmem_limit_bytes=48 << 20
        ),
        name="exchange",
    )(packed, padded)


def solve_kernel(
    slot_ref, len_ref, block_ref, occ_ref, packed_ref, energy_hbm, own_hbm, padded_hbm, out_hbm,
    m_high, m_low, x_ref, r_ref, rows_buf, out_buf, energy_buf, in_sem, out_sem, energy_sem,
):
    size = x_ref.shape[0]
    tiles, _, width = out_buf.shape
    blocks, _, side = energy_buf.shape
    me = lax.axis_index("occ")
    orbital = slot_ref[me]

    def energy(k):
        return pltpu.make_async_copy(
            energy_hbm.at[block_ref[orbital, k]], energy_buf.at[k], energy_sem.at[k]
        )

    def fetch(t):
        return pltpu.make_async_copy(own_hbm.at[t], rows_buf.at[t], in_sem.at[t])

    def fetch_mine(t):
        return pltpu.make_async_copy(padded_hbm.at[t], rows_buf.at[t], in_sem.at[t])

    def flush(t):
        return pltpu.make_async_copy(
            out_buf.at[t], out_hbm.at[:, pl.ds(t * width, width)], out_sem.at[t]
        )

    for k in range(blocks):
        energy(k).start()
    for t in range(tiles):
        @pl.when(t == me)
        def _():
            fetch_mine(t).start()

        @pl.when(t != me)
        def _():
            fetch(t).start()

    for k in range(blocks):
        energy(k).wait()
    place = 0
    for i in range(blocks):
        column = jnp.broadcast_to(energy_buf[i], (side, side)).T
        for j in range(i + 1):
            level = column + jnp.broadcast_to(energy_buf[j], (side, side)) - 2.0 * occ_ref[orbital]
            part = packed_ref[place * side:(place + 1) * side, :] / level
            x_ref[i * side:(i + 1) * side, j * side:(j + 1) * side] = part
            if j < i:
                x_ref[j * side:(j + 1) * side, i * side:(i + 1) * side] = part.T
            place += 1

    eye = (
        lax.broadcasted_iota(jnp.int32, (size, size), 0)
        == lax.broadcasted_iota(jnp.int32, (size, size), 1)
    ).astype(F32)
    amplitude = x_ref[...]
    trace = jnp.sum(amplitude * eye)
    live = (side * len_ref[orbital]).astype(F32)
    level_shift = LEVEL_RATIO * (trace / live + EPSILON)
    row_sum = jnp.max(jnp.sum(jnp.abs(amplitude), axis=0, keepdims=True))
    upper = level_shift + 1.01 * jnp.minimum(row_sum, 1.01 * trace)
    unit = 2.0 / (level_shift + upper)
    start = level_shift * unit
    scaled = (amplitude + level_shift * eye) * unit
    high, low = split(scaled)
    m_high[...] = high
    m_low[...] = low

    def factor(rho):
        return 2.0 / (1.0 + rho * (2.0 - rho))

    def advance(rho):
        return factor(rho) * rho * (2.0 - rho)

    x_ref[...] = factor(start) * (2.0 * eye - scaled)

    def quick(rho):
        x = x_ref[...]
        xb = x.astype(BF16)
        t = dot(m_high[...], xb)
        x_ref[...] = factor(rho) * (2.0 * x - dot(xb, t.astype(BF16)))
        return advance(rho)

    rho = lax.while_loop(lambda rho: rho < 0.95, quick, advance(start))
    del rho

    def times_m(x):
        xh, xl = split(x)
        mh = m_high[...]
        return dot(mh, xh) + (dot(mh, xl) + dot(m_low[...], xh))

    def residual():
        r = eye_again() - times_m(x_ref[...])
        r_ref[...] = r
        return jnp.sum(r * r)

    def eye_again():
        return (
            lax.broadcasted_iota(jnp.int32, (size, size), 0)
            == lax.broadcasted_iota(jnp.int32, (size, size), 1)
        ).astype(F32)

    def x_times(value):
        xh, xl = split(x_ref[...])
        vh, vl = split(value)
        return dot(xh, vh) + (dot(xh, vl) + dot(xl, vh))

    norm = residual()

    def careful(rho):
        x_ref[...] = factor(rho) * (2.0 * x_ref[...] - x_times(times_m(x_ref[...])))
        return advance(rho)

    def restart(_):
        x_ref[...] = eye_again()
        lax.while_loop(lambda rho: rho < 0.9999, careful, start)
        return residual()

    norm = lax.cond(norm < 0.9, lambda n: n, restart, norm)

    def refine(state):
        _, step = state
        x_ref[...] = x_ref[...] + x_times(r_ref[...])
        return residual(), step + 1

    lax.while_loop(
        lambda state: jnp.logical_and(state[0] > 1e-6, state[1] < 12), refine, (norm, 0)
    )
    x = x_ref[...] + x_times(r_ref[...])
    projector = (eye_again() - (level_shift * unit) * x).astype(BF16)
    m_high[...] = projector
    for t in range(tiles):
        fetch(t).wait()
        out_buf[t] = dot(m_high[...], rows_buf[t]).astype(BF16)
        flush(t).start()
    for t in range(tiles):
        flush(t).wait()


def solve_and_project(slot_orbital, domain_len, domain_blocks, occ_energy, packed, table, own, padded):
    groups, size, width = own.shape
    blocks = domain_blocks.shape[1]
    side = size // blocks
    vmem = pl.BlockSpec(memory_space=pltpu.VMEM)
    smem = pl.BlockSpec(memory_space=pltpu.SMEM)
    hbm = pl.BlockSpec(memory_space=pl.ANY)
    return pl.pallas_call(
        solve_kernel,
        out_shape=jax.ShapeDtypeStruct((size, groups * width), BF16),
        in_specs=[smem] * 4 + [vmem] + [hbm] * 3,
        out_specs=hbm,
        scratch_shapes=[
            pltpu.VMEM((size, size), BF16),
            pltpu.VMEM((size, size), BF16),
            pltpu.VMEM((size, size), F32),
            pltpu.VMEM((size, size), F32),
            pltpu.VMEM((groups, size, width), BF16),
            pltpu.VMEM((groups, size, width), BF16),
            pltpu.VMEM((blocks, 1, side), F32),
            pltpu.SemaphoreType.DMA((groups,)),
            pltpu.SemaphoreType.DMA((groups,)),
            pltpu.SemaphoreType.DMA((blocks,)),
        ],
        compiler_params=pltpu.CompilerParams(vmem_limit_bytes=48 << 20),
        name="solve",
    )(slot_orbital, domain_len, domain_blocks, occ_energy, packed, table, own, padded)


def solution(mesh):
    n_aux = mesh.shape["aux"]

    def local(pair_ints, domain_len, domain_blocks, slot_orbital, virt_energy, occ_energy):
        blocks = domain_blocks.shape[1]
        padded, packed = gather_and_gram(slot_orbital, domain_len, pair_ints, blocks)
        gram, own = exchange(packed, padded, n_aux)
        table = virt_energy.reshape(-1, 1, pair_ints.shape[1])
        return solve_and_project(
            slot_orbital, domain_len, domain_blocks, occ_energy, gram, table, own, padded
        )[None]

    placed = (P(None, None, ("aux", "occ")), P(), P(), P(), P(), P())
    return jax.shard_map(
        local, mesh=mesh, in_specs=placed, out_specs=P("occ", None, "aux"), check_vma=False
    )
```

time: 157 us -> 75.6 us (0.48)
  waiting for transfers between devices: 65.8 us -> 0 us
  Pallas kernels: 14.5 us -> 73.5 us
  blocking collectives: 35.4 us -> 0 us
  between operations: 16.2 us -> 0.06 us
  local copies, waits for them, and re-layouts: 17.7 us -> 1.76 us
  other arithmetic: 4.58 us -> 0 us
  matrix products: 2.57 us -> 0 us
    psum x1 -> x0, waiting for transfers between devices: 65.8 us -> none  [local(): lax.psum(jnp.einsum('ac,bc->ab', own_rows, own_rows, preferred_element_ty...]
    pallas_call x1 -> x3, Pallas kernels: 14.5 us -> 73.5 us  [the longest x1 51.7 us: exchange(): pl.pallas_call(functools.partial(exchange_kernel, ny, nx, nz), out_shape=...]
    all_to_all x1 -> x0, blocking collectives: 35.4 us -> none  [local(): lax.all_to_all(padded, 'occ', split_axis=0, concat_axis=2, tiled=True)[0]]
    gather x3 -> x0, local copies, waits for them, and re-layouts: 5.2 us -> none  [the longest x1 2.36 us: local(): picked = jnp.take(pair_ints, starts.reshape(-1), axis=0)]
    unnamed x21 -> x12, local copies, waits for them, and re-layouts: 6.56 us -> 1.76 us
    all_to_all x1 -> x0, local copies, waits for them, and re-layouts: 3.76 us -> none  [local(): lax.all_to_all(padded, 'occ', split_axis=0, concat_axis=2, tiled=True)[0]]
    select_n x6 -> x0, other arithmetic: 3.66 us -> none  [the longest x1 2.1 us: local(): jnp.where(live_mask.reshape(-1)[:, None, None], picked, jnp.zeros_like(pi...]
    dot_general x1 -> x0, matrix products: 2.57 us -> none  [local(): jnp.einsum('ac,bc->ab', own_rows, own_rows, preferred_element_type=F32)]
  transfers between devices with their start and end apart: 1 -> 0, of which waited for: 1 -> 0; matrix products, arithmetic and copies ran while one was open for 6% -> 0% of each run, Pallas kernels for 0% -> 0%
where the time goes in v2:
time: 75.6 us; the launch traced here: 75.3 us
  Pallas kernels  73.5 us (97%)
  local copies, waits for them, and re-layouts  1.76 us (2%)
    pallas_call x1, Pallas kernels, exchange(): pl.pallas_call(functools.partial(exchange_kernel, ny, nx, nz), out_shape=...  51.7 us
    pallas_call x1, Pallas kernels, solve_and_project(): pl.pallas_call(solve_kernel, out_shape=jax.ShapeDtypeStruct((size, groups...  15.8 us
    pallas_call x1, Pallas kernels, gather_and_gram(): pl.pallas_call(gather_kernel, out_shape=(jax.ShapeDtypeStruct((groups, bl...  5.96 us
    unnamed x12, local copies, waits for them, and re-layouts  1.76 us

profile of v2, /device:TPU:0, one launch (start us, length us, event | category | flops | bytes accessed | tf_op | source)
XLA Modules:
  0.0 75.3 jit_solution(4972731304862578287)
XLA Ops:
  0.0 6.0 %gather.1 = (bf16[4,512,640]{2,1,0:T(8,128)(2,1)}, f32[4,1280,128]{2,1,0:T(8,128)}) custom-call(s32[4]{0:T(128)} %slot_ref.3, s32[4]{0:T(128)} %len_ref.3, bf16[16,128,640]{2,1,0:T(8,128)(2,1)} %pair_ref.1), custom_call_target="tpu_custom_call" | custom-call | tf_op jit(solution)/shard_map/gather/pallas_call | solution.py:48
  6.0 0.0 copy-start
  6.0 1.7 %copy-done = f32[4,1280,128]{2,1,0:T(8,128)S(1)} copy-done((f32[4,1280,128]{2,1,0:T(8,128)S(1)}, f32[4,1280,128]{2,1,0:T(8,128)}, u32[]{:S(2)}) %copy-start) | copy-done | bytes 2621464
  7.7 0.0 copy-start.1
  7.7 0.0 copy-start.2
  7.7 0.0 copy-start.3
  7.7 0.0 copy-start.4
  7.7 0.0 copy-start.5
  7.7 51.7 %exchange.1 = (f32[1280,128]{1,0:T(8,128)S(1)}, bf16[4,512,640]{2,1,0:T(8,128)(2,1)S(1)}) custom-call(f32[4,1280,128]{2,1,0:T(8,128)S(1)} %copy-done, bf16[4,512,640]{2,1,0:T(8,128)(2,1)} %get-tuple-element.10.rows_ref.padded_hbm), custom_call_target="tpu_custom_call" | custom-call | tf_op jit(solution)/shard_map/exchange/pallas_call | solution.py:250
  59.5 0.0 copy-done.1
  59.5 0.0 copy-done.2
  59.5 0.0 copy-done.3
  59.5 0.0 copy-done.4
  59.5 0.0 copy-done.5
  59.5 15.8 %solve.1 = bf16[512,2560]{1,0:T(8,128)(2,1)} custom-call(s32[4]{0:T(128)S(1)} %copy-done.3, s32[4]{0:T(128)S(1)} %copy-done.4, s32[4,4]{1,0:T(4,128)S(1)} %copy-done.2, f32[4]{0:T(128)S(1)} %copy-done.5, f32[1280,128]{1,0:T(8,128)S(1)} %get-tuple-element.11.packed_ref, f32[704,1,128]{2,1,0:T(1,128)S(1)} %bitcast.2, ...), custom_call_target="tpu_custom_call" | custom-call | tf_op jit(solution)/shard_map/solve/pallas_call | solution.py:419
Async XLA Ops:
  6.0 1.7 %copy-start = (f32[4,1280,128]{2,1,0:T(8,128)S(1)}, f32[4,1280,128]{2,1,0:T(8,128)}, u32[]{:S(2)}) copy-start(f32[4,1280,128]{2,1,0:T(8,128)} %get-tuple-element.9.part_ref) | copy-start | bytes 7864324
  7.7 51.8 %copy-start.1 = (f32[90112]{0:T(1024)S(1)}, f32[90112]{0:T(1024)}, u32[]{:S(2)}) copy-start(f32[90112]{0:T(1024)} %param.10) | copy-start | bytes 1081348
  7.7 51.8 %copy-start.2 = (s32[4,4]{1,0:T(4,128)S(1)}, s32[4,4]{1,0:T(4,128)}, u32[]{:S(2)}) copy-start(s32[4,4]{1,0:T(4,128)} %block_ref.1) | copy-start | bytes 196
  7.7 51.8 %copy-start.3 = (s32[4]{0:T(128)S(1)}, s32[4]{0:T(128)}, u32[]{:S(2)}) copy-start(s32[4]{0:T(128)} %slot_ref.3) | copy-start | bytes 52
  7.7 51.8 %copy-start.4 = (s32[4]{0:T(128)S(1)}, s32[4]{0:T(128)}, u32[]{:S(2)}) copy-start(s32[4]{0:T(128)} %len_ref.3) | copy-start | bytes 52
  7.7 51.8 %copy-start.5 = (f32[4]{0:T(128)S(1)}, f32[4]{0:T(128)}, u32[]{:S(2)}) copy-start(f32[4]{0:T(128)} %occ_ref.1) | copy-start | bytes 52

commit v3 on v2

--- a/solution.py
+++ b/solution.py
@@ -22,57 +22,14 @@
     return jnp.dot(a, b, preferred_element_type=F32)
 
 
-def gather_kernel(slot_ref, len_ref, pair_ref, padded_ref, packed_ref):
-    blocks, size, cols = pair_ref.shape
-    length = len_ref[slot_ref[pl.program_id(0)]]
-    for k in range(blocks):
-        rows = pair_ref[k]
-        padded_ref[0, k * size:(k + 1) * size, :] = jnp.where(k < length, rows, jnp.zeros_like(rows))
-    place = 0
-    for i in range(blocks):
-        band = lax.dot_general(
-            padded_ref[0, i * size:(i + 1) * size, :],
-            padded_ref[0, :(i + 1) * size, :],
-            (((1,), (1,)), ((), ())),
-            preferred_element_type=F32,
-        )
-        for j in range(i + 1):
-            packed_ref[0, place * size:(place + 1) * size, :] = band[:, j * size:(j + 1) * size]
-            place += 1
-
-
-def gather_and_gram(slot_orbital, domain_len, pair_ints, blocks):
-    groups = slot_orbital.shape[0]
-    _, size, cols = pair_ints.shape
-    packed = blocks * (blocks + 1) // 2 * size
-    return pl.pallas_call(
-        gather_kernel,
-        out_shape=(
-            jax.ShapeDtypeStruct((groups, blocks * size, cols), BF16),
-            jax.ShapeDtypeStruct((groups, packed, size), F32),
-        ),
-        grid_spec=pltpu.PrefetchScalarGridSpec(
-            num_scalar_prefetch=2,
-            grid=(groups,),
-            in_specs=[pl.BlockSpec((blocks, size, cols), lambda g, slot, _: (slot[g], 0, 0))],
-            out_specs=[
-                pl.BlockSpec((1, blocks * size, cols), lambda g, *_: (g, 0, 0)),
-                pl.BlockSpec((1, packed, size), lambda g, *_: (g, 0, 0)),
-            ],
-        ),
-        compiler_params=pltpu.CompilerParams(dimension_semantics=("arbitrary",)),
-        name="gather",
-    )(slot_orbital, domain_len, pair_ints)
-
-
 MESH = pl.DeviceIdType.MESH
 
 
 def exchange_kernel(
-    ny, nx, nz, part_ref, rows_ref, gram_ref, own_ref,
-    core_buf, y_out, y_in, x_out, x_in, z_out, z_in,
+    ny, nx, nz, slot_ref, len_ref, pair_hbm, gram_ref, own_ref,
+    pair_buf, pad_buf, part_ref, core_buf, y_out, y_in, x_out, x_in, z_out, z_in,
     core_ss, core_rs, y_ss, y_rs, x_ss, x_rs, z_ss, z_rs,
-    gz_ss, gz_rs, gx_ss, gx_rs, row_ss, row_rs,
+    gz_ss, gz_rs, gx_ss, gx_rs, row_ss, row_rs, pair_sem, mine_sem,
 ):
     occ, aux = lax.axis_index("occ"), lax.axis_index("aux")
     y, core = lax.div(occ, 2), lax.rem(occ, 2)
@@ -102,6 +59,16 @@
             device_id=(to_occ, to_aux), device_id_type=MESH,
         )
 
+    groups, domain, _ = pad_buf.shape
+    size = pair_buf.shape[1]
+    blocks = domain // size
+
+    def load(g):
+        span = pl.ds(g * blocks, blocks)
+        return pltpu.make_async_copy(pair_hbm.at[span], pair_buf.at[span], pair_sem.at[g])
+
+    for g in range(groups):
+        load(g).start()
     barrier = pltpu.get_barrier_semaphore()
     peers = [(2 * y + other, aux)]
     for d in range(1, ny):
@@ -155,30 +122,69 @@
         part = gram_ref.at[piece_of(lax.rem(x + nx - e, nx), lax.rem(z + nz - f, nz))]
         return copy(part, part, gx_ss.at[e, f], gx_rs.at[e, f], occ, z * nx + at_x(e))
 
-    def row_copy(d, swap):
+    half = domain // 2
+
+    def row_copy(d, swap, h):
         target = 2 * at_y(d) + (other if swap else core)
-        return copy(
-            rows_ref.at[target], own_ref.at[occ], row_ss.at[d, swap], row_rs.at[d, swap], target, aux
-        )
-
-    def row_in(d, swap):
+        span = pl.ds(h * half, half)
+        return copy(
+            pad_buf.at[target, span], own_ref.at[occ, span],
+            row_ss.at[d, swap, h], row_rs.at[d, swap, h], target, aux,
+        )
+
+    def row_in(d, swap, h):
         source = 2 * lax.rem(y + ny - d, ny) + (other if swap else core)
-        return copy(
-            rows_ref.at[source], own_ref.at[source], row_ss.at[d, swap], row_rs.at[d, swap], source, aux
-        )
-
-    row_moves = [(d, s) for d in range(1, ny) for s in (0, 1)] + [(0, 1)]
-
+        span = pl.ds(h * half, half)
+        return copy(
+            pad_buf.at[source, span], own_ref.at[source, span],
+            row_ss.at[d, swap, h], row_rs.at[d, swap, h], source, aux,
+        )
+
+    def gather(g):
+        orbital = slot_ref[g]
+        length = len_ref[orbital]
+        for k in range(blocks):
+            rows = pair_buf[orbital * blocks + k]
+            pad_buf[g, k * size:(k + 1) * size, :] = jnp.where(k < length, rows, jnp.zeros_like(rows))
+
+    def gram(g):
+        place = 0
+        for i in range(blocks):
+            band = lax.dot_general(
+                pad_buf[g, i * size:(i + 1) * size, :],
+                pad_buf[g, :(i + 1) * size, :],
+                (((1,), (1,)), ((), ())),
+                preferred_element_type=F32,
+            )
+            for j in range(i + 1):
+                part_ref[g, place * size:(place + 1) * size, :] = band[:, j * size:(j + 1) * size]
+                place += 1
+
+    early = [(d, 0, 0) for d in range(1, ny)]
+    late = [(d, 0, 1) for d in range(1, ny)] + [(d, 1, h) for d in far_y for h in (0, 1)]
+    for g in range(groups):
+        load(g).wait()
+    for d in range(1, ny):
+        gather(2 * at_y(d) + core)
+        row_copy(d, 0, 0).start()
     for d in far_y:
+        gather(2 * at_y(d) + other)
+        gram(2 * at_y(d) + other)
         for e in far_x:
             core_copy(d, e).start()
+    for d in range(1, ny):
+        gram(2 * at_y(d) + core)
     for e in far_x:
         for d in range(1, ny):
             core_copy(d, e).wait_recv()
             y_out[d, chunk_of(e), :] = part_ref[2 * at_y(d) + core, chunk_of(e), :] + core_buf[d, chunk_of(e), :]
             y_copy(d, e).start()
-    for move in row_moves:
+    for move in late:
         row_copy(*move).start()
+    gather(occ)
+    mine = pltpu.make_async_copy(pad_buf.at[occ], own_ref.at[occ], mine_sem)
+    mine.start()
+    gram(occ)
     for e in far_x:
         core_copy(0, e).wait_recv()
         for d in range(1, ny):
@@ -220,8 +226,9 @@
     for e in range(1, nx):
         for f in range(nz):
             gx_in(e, f).wait_recv()
-    for move in row_moves:
+    for move in early + late:
         row_in(*move).wait_recv()
+    mine.wait()
 
     for d in far_y:
         for e in far_x:
@@ -235,27 +242,35 @@
         if f:
             z_copy(f).wait_send()
             gz_copy(f).wait_send()
-    for move in row_moves:
+    for move in early + late:
         row_copy(*move).wait_send()
 
 
-def exchange(packed, padded, n_aux):
-    groups, height, lanes = packed.shape
+def exchange(slot_orbital, domain_len, pair_ints, blocks, n_aux):
+    groups = slot_orbital.shape[0]
+    _, lanes, cols = pair_ints.shape
+    height = blocks * (blocks + 1) // 2 * lanes
     ny = groups // 2
     nx = ny if n_aux % ny == 0 else 1
     nz = n_aux // nx
     piece = height // n_aux
     dma = pltpu.SemaphoreType.DMA
-    sems = [(ny, nx)] * 4 + [(nx, nz)] * 2 + [(nz,)] * 4 + [(nx, nz)] * 2 + [(ny, 2)] * 2
+    sems = [(ny, nx)] * 4 + [(nx, nz)] * 2 + [(nz,)] * 4 + [(nx, nz)] * 2 + [(ny, 2, 2)] * 2
+    sems += [(groups,), ()]
+    smem = pl.BlockSpec(memory_space=pltpu.SMEM)
+    hbm = pl.BlockSpec(memory_space=pl.ANY)
     return pl.pallas_call(
         functools.partial(exchange_kernel, ny, nx, nz),
         out_shape=(
             jax.ShapeDtypeStruct((height, lanes), F32),
-            jax.ShapeDtypeStruct(padded.shape, BF16),
+            jax.ShapeDtypeStruct((groups, blocks * lanes, cols), BF16),
         ),
-        in_specs=[pl.BlockSpec(memory_space=pltpu.VMEM), pl.BlockSpec(memory_space=pl.ANY)],
-        out_specs=[pl.BlockSpec(memory_space=pltpu.VMEM), pl.BlockSpec(memory_space=pl.ANY)],
+        in_specs=[smem, smem, hbm],
+        out_specs=[pl.BlockSpec(memory_space=pltpu.VMEM), hbm],
         scratch_shapes=[
+            pltpu.VMEM(pair_ints.shape, BF16),
+            pltpu.VMEM((groups, blocks * lanes, cols), BF16),
+            pltpu.VMEM((groups, height, lanes), F32),
             pltpu.VMEM((ny, height, lanes), F32),
             pltpu.VMEM((ny, height, lanes), F32),
             pltpu.VMEM((ny, height, lanes), F32),
@@ -268,11 +283,11 @@
             collective_id=0, has_side_effects=True, vmem_limit_bytes=48 << 20
         ),
         name="exchange",
-    )(packed, padded)
+    )(slot_orbital, domain_len, pair_ints)
 
 
 def solve_kernel(
-    slot_ref, len_ref, block_ref, occ_ref, packed_ref, energy_hbm, own_hbm, padded_hbm, out_hbm,
+    slot_ref, len_ref, block_ref, occ_ref, packed_ref, energy_hbm, own_hbm, out_hbm,
     m_high, m_low, x_ref, r_ref, rows_buf, out_buf, energy_buf, in_sem, out_sem, energy_sem,
 ):
     size = x_ref.shape[0]
@@ -289,9 +304,6 @@
     def fetch(t):
         return pltpu.make_async_copy(own_hbm.at[t], rows_buf.at[t], in_sem.at[t])
 
-    def fetch_mine(t):
-        return pltpu.make_async_copy(padded_hbm.at[t], rows_buf.at[t], in_sem.at[t])
-
     def flush(t):
         return pltpu.make_async_copy(
             out_buf.at[t], out_hbm.at[:, pl.ds(t * width, width)], out_sem.at[t]
@@ -300,14 +312,7 @@
     for k in range(blocks):
         energy(k).start()
     for t in range(tiles):
-        @pl.when(t == me)
-        def _():
-            fetch_mine(t).start()
-
-        @pl.when(t != me)
-        def _():
-            fetch(t).start()
-
+        fetch(t).start()
     for k in range(blocks):
         energy(k).wait()
     place = 0
@@ -409,7 +414,7 @@
         flush(t).wait()
 
 
-def solve_and_project(slot_orbital, domain_len, domain_blocks, occ_energy, packed, table, own, padded):
+def solve_and_project(slot_orbital, domain_len, domain_blocks, occ_energy, packed, table, own):
     groups, size, width = own.shape
     blocks = domain_blocks.shape[1]
     side = size // blocks
@@ -419,7 +424,7 @@
     return pl.pallas_call(
         solve_kernel,
         out_shape=jax.ShapeDtypeStruct((size, groups * width), BF16),
-        in_specs=[smem] * 4 + [vmem] + [hbm] * 3,
+        in_specs=[smem] * 4 + [vmem] + [hbm] * 2,
         out_specs=hbm,
         scratch_shapes=[
             pltpu.VMEM((size, size), BF16),
@@ -435,7 +440,7 @@
         ],
         compiler_params=pltpu.CompilerParams(vmem_limit_bytes=48 << 20),
         name="solve",
-    )(slot_orbital, domain_len, domain_blocks, occ_energy, packed, table, own, padded)
+    )(slot_orbital, domain_len, domain_blocks, occ_energy, packed, table, own)
 
 
 def solution(mesh):
@@ -443,11 +448,10 @@
 
     def local(pair_ints, domain_len, domain_blocks, slot_orbital, virt_energy, occ_energy):
         blocks = domain_blocks.shape[1]
-        padded, packed = gather_and_gram(slot_orbital, domain_len, pair_ints, blocks)
-        gram, own = exchange(packed, padded, n_aux)
+        gram, own = exchange(slot_orbital, domain_len, pair_ints, blocks, n_aux)
         table = virt_energy.reshape(-1, 1, pair_ints.shape[1])
         return solve_and_project(
-            slot_orbital, domain_len, domain_blocks, occ_energy, gram, table, own, padded
+            slot_orbital, domain_len, domain_blocks, occ_energy, gram, table, own
         )[None]
 
     placed = (P(None, None, ("aux", "occ")), P(), P(), P(), P(), P())

time: 75.6 us -> 70 us (0.926)
  Pallas kernels: 73.5 us -> 66.3 us
  local copies, waits for them, and re-layouts: 1.76 us -> 3.07 us
    pallas_call x1 -> x0, Pallas kernels: 5.96 us -> none  [gather_and_gram(): pl.pallas_call(gather_kernel, out_shape=(jax.ShapeDtypeStruct((groups, bl...]
    pallas_call x1, Pallas kernels: 51.7 us -> 50.3 us  [exchange(): pl.pallas_call(functools.partial(exchange_kernel, ny, nx, nz), out_shape=...]
    unnamed x12, local copies, waits for them, and re-layouts: 1.76 us -> 3.07 us
where the time goes in v3:
time: 70 us; the launch traced here: 69.4 us
  Pallas kernels  66.3 us (95%)
  local copies, waits for them, and re-layouts  3.07 us (4%)
    pallas_call x1, Pallas kernels, exchange(): pl.pallas_call(functools.partial(exchange_kernel, ny, nx, nz), out_shape=...  50.3 us
    pallas_call x1, Pallas kernels, solve_and_project(): pl.pallas_call(solve_kernel, out_shape=jax.ShapeDtypeStruct((size, groups...  16 us
    unnamed x12, local copies, waits for them, and re-layouts  3.07 us

profile of v3, /device:TPU:0, one launch (start us, length us, event | category | flops | bytes accessed | tf_op | source)
XLA Modules:
  0.0 69.4 jit_solution(10951648950332519626)
XLA Ops:
  0.0 0.0 copy-start.5
  0.0 0.0 copy-start
  0.0 1.8 %copy-done = bf16[16,128,640]{2,1,0:T(8,128)(2,1)S(1)} copy-done((bf16[16,128,640]{2,1,0:T(8,128)(2,1)S(1)}, bf16[16,128,640]{2,1,0:T(8,128)(2,1)}, u32[]{:S(2)}) %copy-start) | copy-done | bytes 2621464
  1.8 0.0 copy-start.3
  1.8 0.7 copy-done.3
  2.4 0.0 copy-start.4
  2.4 0.7 copy-done.4
  3.1 0.0 copy-start.1
  3.1 0.0 copy-start.2
  3.1 50.3 %exchange.1 = (f32[1280,128]{1,0:T(8,128)S(1)}, bf16[4,512,640]{2,1,0:T(8,128)(2,1)S(1)}) custom-call(s32[4]{0:T(128)S(1)} %copy-done.3, s32[4]{0:T(128)S(1)} %copy-done.4, bf16[16,128,640]{2,1,0:T(8,128)(2,1)S(1)} %copy-done), custom_call_target="tpu_custom_call" | custom-call | tf_op jit(solution)/shard_map/exchange/pallas_call | solution.py:262
  53.4 0.0 copy-done.5
  53.4 0.0 copy-done.1
  53.4 0.0 copy-done.2
  53.4 16.0 %solve.1 = bf16[512,2560]{1,0:T(8,128)(2,1)} custom-call(s32[4]{0:T(128)S(1)} %copy-done.3, s32[4]{0:T(128)S(1)} %copy-done.4, s32[4,4]{1,0:T(4,128)S(1)} %copy-done.2, f32[4]{0:T(128)S(1)} %copy-done.5, f32[1280,128]{1,0:T(8,128)S(1)} %get-tuple-element.7.packed_ref, f32[704,1,128]{2,1,0:T(1,128)S(1)} %bitcast.2, ...), custom_call_target="tpu_custom_call" | custom-call | tf_op jit(solution)/shard_map/solve/pallas_call | solution.py:424
Async XLA Ops:
  0.0 53.4 %copy-start.5 = (f32[4]{0:T(128)S(1)}, f32[4]{0:T(128)}, u32[]{:S(2)}) copy-start(f32[4]{0:T(128)} %occ_ref.1) | copy-start | bytes 52
  0.0 1.8 %copy-start = (bf16[16,128,640]{2,1,0:T(8,128)(2,1)S(1)}, bf16[16,128,640]{2,1,0:T(8,128)(2,1)}, u32[]{:S(2)}) copy-start(bf16[16,128,640]{2,1,0:T(8,128)(2,1)} %pair_hbm.1) | copy-start | bytes 7864324
  1.8 0.7 copy-start.3
  2.4 0.7 copy-start.4
  3.1 50.3 %copy-start.1 = (f32[90112]{0:T(1024)S(1)}, f32[90112]{0:T(1024)}, u32[]{:S(2)}) copy-start(f32[90112]{0:T(1024)} %param.10) | copy-start | bytes 1081348
  3.1 50.3 %copy-start.2 = (s32[4,4]{1,0:T(4,128)S(1)}, s32[4,4]{1,0:T(4,128)}, u32[]{:S(2)}) copy-start(s32[4,4]{1,0:T(4,128)} %block_ref.1) | copy-start | bytes 196

commit v4 on v3

--- a/solution.py
+++ b/solution.py
@@ -22,12 +22,121 @@
     return jnp.dot(a, b, preferred_element_type=F32)
 
 
+def diagonal(size):
+    return (
+        lax.broadcasted_iota(jnp.int32, (size, size), 0)
+        == lax.broadcasted_iota(jnp.int32, (size, size), 1)
+    ).astype(F32)
+
+
+def factor(rho):
+    return 2.0 / (1.0 + rho * (2.0 - rho))
+
+
+def advance(rho):
+    return factor(rho) * rho * (2.0 - rho)
+
+
+def prepare(energy, blocks, occ_level, live, packed_ref, m_high, m_low, x_ref):
+    size = x_ref.shape[0]
+    side = size // blocks
+    place = 0
+    for i in range(blocks):
+        column = jnp.broadcast_to(energy(i), (side, side)).T
+        for j in range(i + 1):
+            level = column + jnp.broadcast_to(energy(j), (side, side)) - 2.0 * occ_level
+            part = packed_ref[place * side:(place + 1) * side, :] / level
+            x_ref[i * side:(i + 1) * side, j * side:(j + 1) * side] = part
+            if j < i:
+                x_ref[j * side:(j + 1) * side, i * side:(i + 1) * side] = part.T
+            place += 1
+    eye = diagonal(size)
+    amplitude = x_ref[...]
+    trace = jnp.sum(amplitude * eye)
+    level_shift = LEVEL_RATIO * (trace / live + EPSILON)
+    row_sum = jnp.max(jnp.sum(jnp.abs(amplitude), axis=0, keepdims=True))
+    upper = level_shift + 1.01 * jnp.minimum(row_sum, 1.01 * trace)
+    unit = 2.0 / (level_shift + upper)
+    start = level_shift * unit
+    scaled = (amplitude + level_shift * eye) * unit
+    high, low = split(scaled)
+    m_high[...] = high
+    m_low[...] = low
+    x_ref[...] = factor(start) * (2.0 * eye - scaled)
+    return start
+
+
+def times_m(m_high, m_low, x):
+    xh, xl = split(x)
+    mh = m_high[...]
+    return dot(mh, xh) + (dot(mh, xl) + dot(m_low[...], xh))
+
+
+def x_times(x, value):
+    xh, xl = split(x)
+    vh, vl = split(value)
+    return dot(xh, vh) + (dot(xh, vl) + dot(xl, vh))
+
+
+def residual(m_high, m_low, x_ref, r_ref):
+    r = diagonal(x_ref.shape[0]) - times_m(m_high, m_low, x_ref[...])
+    r_ref[...] = r
+    return jnp.sum(r * r)
+
+
+def quick(m_high, x_ref, rho):
+    x = x_ref[...]
+    xb = x.astype(BF16)
+    t = dot(m_high[...], xb)
+    x_ref[...] = factor(rho) * (2.0 * x - dot(xb, t.astype(BF16)))
+    return advance(rho)
+
+
+QUICK_STEPS = 5
+RESIDUAL_BOUND = 1e-6
+
+
+def invert_fixed(start, m_high, m_low, x_ref, r_ref):
+    lax.fori_loop(0, QUICK_STEPS, lambda _, rho: quick(m_high, x_ref, rho), advance(start))
+    residual(m_high, m_low, x_ref, r_ref)
+    x = x_ref[...]
+    x_ref[...] = x + dot(x.astype(BF16), r_ref[...].astype(BF16))
+    residual(m_high, m_low, x_ref, r_ref)
+    x = x_ref[...]
+    x_ref[...] = x + x_times(x, r_ref[...])
+    norm = residual(m_high, m_low, x_ref, r_ref)
+    x = x_ref[...]
+    x = x + dot(x.astype(BF16), r_ref[...].astype(BF16))
+    return diagonal(x.shape[0]) - start * x, norm
+
+
+def invert_checked(start, m_high, m_low, x_ref, r_ref):
+    def careful(rho):
+        x = x_ref[...]
+        x_ref[...] = factor(rho) * (2.0 * x - x_times(x, times_m(m_high, m_low, x)))
+        return advance(rho)
+
+    lax.while_loop(lambda rho: rho < 0.9999, careful, advance(start))
+
+    def refine(state):
+        x_ref[...] = x_ref[...] + x_times(x_ref[...], r_ref[...])
+        return residual(m_high, m_low, x_ref, r_ref), state[1] + 1
+
+    lax.while_loop(
+        lambda state: jnp.logical_and(state[0] > RESIDUAL_BOUND, state[1] < 12),
+        refine,
+        (residual(m_high, m_low, x_ref, r_ref), 0),
+    )
+    x = x_ref[...] + x_times(x_ref[...], r_ref[...])
+    return diagonal(x.shape[0]) - start * x
+
+
 MESH = pl.DeviceIdType.MESH
 
 
 def exchange_kernel(
-    ny, nx, nz, slot_ref, len_ref, pair_hbm, gram_ref, own_ref,
-    pair_buf, pad_buf, part_ref, core_buf, y_out, y_in, x_out, x_in, z_out, z_in,
+    ny, nx, nz, slot_ref, len_ref, block_ref, occ_ref, energy_ref, pair_hbm,
+    gram_ref, own_ref, filter_ref, norm_ref, m_high, m_low, x_ref, r_ref, pair_buf, pad_buf, part_ref, core_buf, y_out, y_in, x_out, x_in, z_out, z_in,
     core_ss, core_rs, y_ss, y_rs, x_ss, x_rs, z_ss, z_rs,
     gz_ss, gz_rs, gx_ss, gx_rs, row_ss, row_rs, pair_sem, mine_sem,
 ):
@@ -226,6 +335,14 @@
     for e in range(1, nx):
         for f in range(nz):
             gx_in(e, f).wait_recv()
+    orbital = slot_ref[occ]
+    start = prepare(
+        lambda k: energy_ref[block_ref[orbital, k]], blocks, occ_ref[orbital],
+        (size * len_ref[orbital]).astype(F32), gram_ref, m_high, m_low, x_ref,
+    )
+    projector, norm = invert_fixed(start, m_high, m_low, x_ref, r_ref)
+    filter_ref[...] = projector.astype(BF16)
+    norm_ref[...] = jnp.full(norm_ref.shape, norm, F32)
     for move in early + late:
         row_in(*move).wait_recv()
     mine.wait()
@@ -246,7 +363,9 @@
         row_copy(*move).wait_send()
 
 
-def exchange(slot_orbital, domain_len, pair_ints, blocks, n_aux):
+def exchange(slot_orbital, domain_len, domain_blocks, occ_energy, table, pair_ints, n_aux):
+    blocks = domain_blocks.shape[1]
+    domain = blocks * pair_ints.shape[1]
     groups = slot_orbital.shape[0]
     _, lanes, cols = pair_ints.shape
     height = blocks * (blocks + 1) // 2 * lanes
@@ -258,16 +377,22 @@
     sems = [(ny, nx)] * 4 + [(nx, nz)] * 2 + [(nz,)] * 4 + [(nx, nz)] * 2 + [(ny, 2, 2)] * 2
     sems += [(groups,), ()]
     smem = pl.BlockSpec(memory_space=pltpu.SMEM)
-    hbm = pl.BlockSpec(memory_space=pl.ANY)
+    vmem = pl.BlockSpec(memory_space=pltpu.VMEM)
     return pl.pallas_call(
         functools.partial(exchange_kernel, ny, nx, nz),
         out_shape=(
             jax.ShapeDtypeStruct((height, lanes), F32),
-            jax.ShapeDtypeStruct((groups, blocks * lanes, cols), BF16),
+            jax.ShapeDtypeStruct((groups, domain, cols), BF16),
+            jax.ShapeDtypeStruct((domain, domain), BF16),
+            jax.ShapeDtypeStruct((8, lanes), F32),
         ),
-        in_specs=[smem, smem, hbm],
-        out_specs=[pl.BlockSpec(memory_space=pltpu.VMEM), hbm],
+        in_specs=[smem] * 4 + [vmem, pl.BlockSpec(memory_space=pltpu.HBM)],
+        out_specs=[vmem] * 4,
         scratch_shapes=[
+            pltpu.VMEM((domain, domain), BF16),
+            pltpu.VMEM((domain, domain), BF16),
+            pltpu.VMEM((domain, domain), F32),
+            pltpu.VMEM((domain, domain), F32),
             pltpu.VMEM(pair_ints.shape, BF16),
             pltpu.VMEM((groups, blocks * lanes, cols), BF16),
             pltpu.VMEM((groups, height, lanes), F32),
@@ -283,175 +408,87 @@
             collective_id=0, has_side_effects=True, vmem_limit_bytes=48 << 20
         ),
         name="exchange",
-    )(slot_orbital, domain_len, pair_ints)
-
-
-def solve_kernel(
-    slot_ref, len_ref, block_ref, occ_ref, packed_ref, energy_hbm, own_hbm, out_hbm,
-    m_high, m_low, x_ref, r_ref, rows_buf, out_buf, energy_buf, in_sem, out_sem, energy_sem,
+    )(slot_orbital, domain_len, domain_blocks, occ_energy, table, pair_ints)
+
+
+def project_kernel(
+    slot_ref, len_ref, block_ref, occ_ref, packed_ref, own_ref, filter_ref, norm_ref, energy_hbm, out_hbm,
+    m_high, m_low, x_ref, r_ref, out_buf, energy_buf, out_sem, energy_sem,
 ):
-    size = x_ref.shape[0]
     tiles, _, width = out_buf.shape
     blocks, _, side = energy_buf.shape
-    me = lax.axis_index("occ")
-    orbital = slot_ref[me]
-
-    def energy(k):
-        return pltpu.make_async_copy(
-            energy_hbm.at[block_ref[orbital, k]], energy_buf.at[k], energy_sem.at[k]
-        )
-
-    def fetch(t):
-        return pltpu.make_async_copy(own_hbm.at[t], rows_buf.at[t], in_sem.at[t])
+    orbital = slot_ref[lax.axis_index("occ")]
+    good = jnp.max(norm_ref[...]) < RESIDUAL_BOUND
+
+    @pl.when(good)
+    def _():
+        m_high[...] = filter_ref[...]
+
+    @pl.when(jnp.logical_not(good))
+    def _():
+        def energy(k):
+            return pltpu.make_async_copy(
+                energy_hbm.at[block_ref[orbital, k]], energy_buf.at[k], energy_sem.at[k]
+            )
+
+        for k in range(blocks):
+            energy(k).start()
+        for k in range(blocks):
+            energy(k).wait()
+        live = (side * len_ref[orbital]).astype(F32)
+        start = prepare(
+            lambda k: energy_buf[k], blocks, occ_ref[orbital], live, packed_ref, m_high, m_low, x_ref
+        )
+        m_high[...] = invert_checked(start, m_high, m_low, x_ref, r_ref).astype(BF16)
 
     def flush(t):
         return pltpu.make_async_copy(
             out_buf.at[t], out_hbm.at[:, pl.ds(t * width, width)], out_sem.at[t]
         )
 
-    for k in range(blocks):
-        energy(k).start()
     for t in range(tiles):
-        fetch(t).start()
-    for k in range(blocks):
-        energy(k).wait()
-    place = 0
-    for i in range(blocks):
-        column = jnp.broadcast_to(energy_buf[i], (side, side)).T
-        for j in range(i + 1):
-            level = column + jnp.broadcast_to(energy_buf[j], (side, side)) - 2.0 * occ_ref[orbital]
-            part = packed_ref[place * side:(place + 1) * side, :] / level
-            x_ref[i * side:(i + 1) * side, j * side:(j + 1) * side] = part
-            if j < i:
-                x_ref[j * side:(j + 1) * side, i * side:(i + 1) * side] = part.T
-            place += 1
-
-    eye = (
-        lax.broadcasted_iota(jnp.int32, (size, size), 0)
-        == lax.broadcasted_iota(jnp.int32, (size, size), 1)
-    ).astype(F32)
-    amplitude = x_ref[...]
-    trace = jnp.sum(amplitude * eye)
-    live = (side * len_ref[orbital]).astype(F32)
-    level_shift = LEVEL_RATIO * (trace / live + EPSILON)
-    row_sum = jnp.max(jnp.sum(jnp.abs(amplitude), axis=0, keepdims=True))
-    upper = level_shift + 1.01 * jnp.minimum(row_sum, 1.01 * trace)
-    unit = 2.0 / (level_shift + upper)
-    start = level_shift * unit
-    scaled = (amplitude + level_shift * eye) * unit
-    high, low = split(scaled)
-    m_high[...] = high
-    m_low[...] = low
-
-    def factor(rho):
-        return 2.0 / (1.0 + rho * (2.0 - rho))
-
-    def advance(rho):
-        return factor(rho) * rho * (2.0 - rho)
-
-    x_ref[...] = factor(start) * (2.0 * eye - scaled)
-
-    def quick(rho):
-        x = x_ref[...]
-        xb = x.astype(BF16)
-        t = dot(m_high[...], xb)
-        x_ref[...] = factor(rho) * (2.0 * x - dot(xb, t.astype(BF16)))
-        return advance(rho)
-
-    rho = lax.while_loop(lambda rho: rho < 0.95, quick, advance(start))
-    del rho
-
-    def times_m(x):
-        xh, xl = split(x)
-        mh = m_high[...]
-        return dot(mh, xh) + (dot(mh, xl) + dot(m_low[...], xh))
-
-    def residual():
-        r = eye_again() - times_m(x_ref[...])
-        r_ref[...] = r
-        return jnp.sum(r * r)
-
-    def eye_again():
-        return (
-            lax.broadcasted_iota(jnp.int32, (size, size), 0)
-            == lax.broadcasted_iota(jnp.int32, (size, size), 1)
-        ).astype(F32)
-
-    def x_times(value):
-        xh, xl = split(x_ref[...])
-        vh, vl = split(value)
-        return dot(xh, vh) + (dot(xh, vl) + dot(xl, vh))
-
-    norm = residual()
-
-    def careful(rho):
-        x_ref[...] = factor(rho) * (2.0 * x_ref[...] - x_times(times_m(x_ref[...])))
-        return advance(rho)
-
-    def restart(_):
-        x_ref[...] = eye_again()
-        lax.while_loop(lambda rho: rho < 0.9999, careful, start)
-        return residual()
-
-    norm = lax.cond(norm < 0.9, lambda n: n, restart, norm)
-
-    def refine(state):
-        _, step = state
-        x_ref[...] = x_ref[...] + x_times(r_ref[...])
-        return residual(), step + 1
-
-    lax.while_loop(
-        lambda state: jnp.logical_and(state[0] > 1e-6, state[1] < 12), refine, (norm, 0)
-    )
-    x = x_ref[...] + x_times(r_ref[...])
-    projector = (eye_again() - (level_shift * unit) * x).astype(BF16)
-    m_high[...] = projector
-    for t in range(tiles):
-        fetch(t).wait()
-        out_buf[t] = dot(m_high[...], rows_buf[t]).astype(BF16)
+        out_buf[t] = dot(m_high[...], own_ref[t]).astype(BF16)
         flush(t).start()
     for t in range(tiles):
         flush(t).wait()
 
 
-def solve_and_project(slot_orbital, domain_len, domain_blocks, occ_energy, packed, table, own):
+def project(slot_orbital, domain_len, domain_blocks, occ_energy, packed, own, projector, norm, table):
     groups, size, width = own.shape
     blocks = domain_blocks.shape[1]
     side = size // blocks
     vmem = pl.BlockSpec(memory_space=pltpu.VMEM)
     smem = pl.BlockSpec(memory_space=pltpu.SMEM)
-    hbm = pl.BlockSpec(memory_space=pl.ANY)
     return pl.pallas_call(
-        solve_kernel,
+        project_kernel,
         out_shape=jax.ShapeDtypeStruct((size, groups * width), BF16),
-        in_specs=[smem] * 4 + [vmem] + [hbm] * 2,
-        out_specs=hbm,
+        in_specs=[smem] * 4 + [vmem] * 4 + [pl.BlockSpec(memory_space=pl.ANY)],
+        out_specs=pl.BlockSpec(memory_space=pl.ANY),
         scratch_shapes=[
             pltpu.VMEM((size, size), BF16),
             pltpu.VMEM((size, size), BF16),
             pltpu.VMEM((size, size), F32),
             pltpu.VMEM((size, size), F32),
             pltpu.VMEM((groups, size, width), BF16),
-            pltpu.VMEM((groups, size, width), BF16),
             pltpu.VMEM((blocks, 1, side), F32),
-            pltpu.SemaphoreType.DMA((groups,)),
             pltpu.SemaphoreType.DMA((groups,)),
             pltpu.SemaphoreType.DMA((blocks,)),
         ],
-        compiler_params=pltpu.CompilerParams(vmem_limit_bytes=48 << 20),
-        name="solve",
-    )(slot_orbital, domain_len, domain_blocks, occ_energy, packed, table, own)
+        compiler_params=pltpu.CompilerParams(vmem_limit_bytes=24 << 20),
+        name="project",
+    )(slot_orbital, domain_len, domain_blocks, occ_energy, packed, own, projector, norm, table)
 
 
 def solution(mesh):
     n_aux = mesh.shape["aux"]
 
     def local(pair_ints, domain_len, domain_blocks, slot_orbital, virt_energy, occ_energy):
-        blocks = domain_blocks.shape[1]
-        gram, own = exchange(slot_orbital, domain_len, pair_ints, blocks, n_aux)
         table = virt_energy.reshape(-1, 1, pair_ints.shape[1])
-        return solve_and_project(
-            slot_orbital, domain_len, domain_blocks, occ_energy, gram, table, own
+        gram, own, projector, norm = exchange(
+            slot_orbital, domain_len, domain_blocks, occ_energy, table, pair_ints, n_aux
+        )
+        return project(
+            slot_orbital, domain_len, domain_blocks, occ_energy, gram, own, projector, norm, table
         )[None]
 
     placed = (P(None, None, ("aux", "occ")), P(), P(), P(), P(), P())

time: 70 us -> 65.4 us (0.934)
  Pallas kernels: 66.3 us -> 61.5 us
    pallas_call x1, Pallas kernels: 16 us -> 3.49 us  [project(): pl.pallas_call(project_kernel, out_shape=jax.ShapeDtypeStruct((size, grou...]
    pallas_call x1, Pallas kernels: 50.3 us -> 58 us  [exchange(): pl.pallas_call(functools.partial(exchange_kernel, ny, nx, nz), out_shape=...]
    unnamed x12 -> x10, local copies, waits for them, and re-layouts: 3.07 us -> 3.63 us
where the time goes in v4:
time: 65.4 us; the launch traced here: 65.2 us
  Pallas kernels  61.5 us (94%)
  local copies, waits for them, and re-layouts  3.63 us (6%)
    pallas_call x1, Pallas kernels, exchange(): pl.pallas_call(functools.partial(exchange_kernel, ny, nx, nz), out_shape=...  58 us
    unnamed x10, local copies, waits for them, and re-layouts  3.63 us
    pallas_call x1, Pallas kernels, project(): pl.pallas_call(project_kernel, out_shape=jax.ShapeDtypeStruct((size, grou...  3.49 us

profile of v4, /device:TPU:0, one launch (start us, length us, event | category | flops | bytes accessed | tf_op | source)
XLA Modules:
  0.0 65.2 jit_solution(14437544166444725464)
XLA Ops:
  0.0 0.0 copy-start
  0.0 1.0 %copy-done = f32[90112]{0:T(1024)S(1)} copy-done((f32[90112]{0:T(1024)S(1)}, f32[90112]{0:T(1024)}, u32[]{:S(2)}) %copy-start) | copy-done | bytes 360472
  1.0 0.0 copy-start.1
  1.0 0.7 %copy-done.1 = s32[4,4]{1,0:T(4,128)S(1)} copy-done((s32[4,4]{1,0:T(4,128)S(1)}, s32[4,4]{1,0:T(4,128)}, u32[]{:S(2)}) %copy-start.1) | copy-done | bytes 88
  1.7 0.0 copy-start.2
  1.7 0.7 %copy-done.2 = s32[4]{0:T(128)S(1)} copy-done((s32[4]{0:T(128)S(1)}, s32[4]{0:T(128)}, u32[]{:S(2)}) %copy-start.2) | copy-done | bytes 40
  2.3 0.0 copy-start.3
  2.3 0.7 %copy-done.3 = s32[4]{0:T(128)S(1)} copy-done((s32[4]{0:T(128)S(1)}, s32[4]{0:T(128)}, u32[]{:S(2)}) %copy-start.3) | copy-done | bytes 40
  3.0 0.0 copy-start.4
  3.0 0.7 %copy-done.4 = f32[4]{0:T(128)S(1)} copy-done((f32[4]{0:T(128)S(1)}, f32[4]{0:T(128)}, u32[]{:S(2)}) %copy-start.4) | copy-done | bytes 40
  3.6 58.0 %exchange.1 = (f32[1280,128]{1,0:T(8,128)S(1)}, bf16[4,512,640]{2,1,0:T(8,128)(2,1)S(1)}, bf16[512,512]{1,0:T(8,128)(2,1)S(1)}, f32[8,128]{1,0:T(8,128)S(1)}) custom-call(s32[4]{0:T(128)S(1)} %copy-done.2, s32[4]{0:T(128)S(1)} %copy-done.3, s32[4,4]{1,0:T(4,128)S(1)} %copy-done.1, f32[4]{0:T(128)S(1)} %copy-done.4, f32[704,1,128]{2,1,0:T(1,128)S(1)} %bitcast.2, ...), custom_call_target="tpu_custom_call" | custom-call | tf_op jit(solution)/shard_map/exchange/pallas_call | solution.py:381
  61.7 3.5 %project.1 = bf16[512,2560]{1,0:T(8,128)(2,1)} custom-call(s32[4]{0:T(128)S(1)} %copy-done.2, s32[4]{0:T(128)S(1)} %copy-done.3, s32[4,4]{1,0:T(4,128)S(1)} %copy-done.1, f32[4]{0:T(128)S(1)} %copy-done.4, f32[1280,128]{1,0:T(8,128)S(1)} %get-tuple-element.9.packed_ref, bf16[4,512,640]{2,1,0:T(8,128)(2,1)S(1)} %get-tuple-element.10.own_ref, ...), custom_call_target="tpu_custom_call" | custom-call | tf_op jit(solution)/shard_map/project/pallas_call | solution.py:462
Async XLA Ops:
  0.0 1.0 %copy-start = (f32[90112]{0:T(1024)S(1)}, f32[90112]{0:T(1024)}, u32[]{:S(2)}) copy-start(f32[90112]{0:T(1024)} %param.10) | copy-start | bytes 1081348
  1.0 0.7 %copy-start.1 = (s32[4,4]{1,0:T(4,128)S(1)}, s32[4,4]{1,0:T(4,128)}, u32[]{:S(2)}) copy-start(s32[4,4]{1,0:T(4,128)} %block_ref.3) | copy-start | bytes 196
  1.7 0.7 %copy-start.2 = (s32[4]{0:T(128)S(1)}, s32[4]{0:T(128)}, u32[]{:S(2)}) copy-start(s32[4]{0:T(128)} %slot_ref.3) | copy-start | bytes 52
  2.3 0.7 %copy-start.3 = (s32[4]{0:T(128)S(1)}, s32[4]{0:T(128)}, u32[]{:S(2)}) copy-start(s32[4]{0:T(128)} %len_ref.3) | copy-start | bytes 52
  3.0 0.7 %copy-start.4 = (f32[4]{0:T(128)S(1)}, f32[4]{0:T(128)}, u32[]{:S(2)}) copy-start(f32[4]{0:T(128)} %occ_ref.3) | copy-start | bytes 52

commit v5 on v4

--- a/solution.py
+++ b/solution.py
@@ -93,6 +93,7 @@
 
 
 QUICK_STEPS = 5
+PIECES = 4
 RESIDUAL_BOUND = 1e-6
 
 
@@ -135,8 +136,9 @@
 
 
 def exchange_kernel(
-    ny, nx, nz, slot_ref, len_ref, block_ref, occ_ref, energy_ref, pair_hbm,
-    gram_ref, own_ref, filter_ref, norm_ref, m_high, m_low, x_ref, r_ref, pair_buf, pad_buf, part_ref, core_buf, y_out, y_in, x_out, x_in, z_out, z_in,
+    ny, nx, nz, slot_hbm, len_hbm, block_hbm, occ_hbm, energy_hbm, pair_hbm,
+    gram_ref, own_ref, filter_ref, norm_ref, slot_ref, len_ref, block_ref, occ_ref, energy_ref, small_sem,
+    m_high, m_low, x_ref, r_ref, pair_buf, pad_buf, part_ref, core_buf, y_out, y_in, x_out, x_in, z_out, z_in,
     core_ss, core_rs, y_ss, y_rs, x_ss, x_rs, z_ss, z_rs,
     gz_ss, gz_rs, gx_ss, gx_rs, row_ss, row_rs, pair_sem, mine_sem,
 ):
@@ -176,8 +178,19 @@
         span = pl.ds(g * blocks, blocks)
         return pltpu.make_async_copy(pair_hbm.at[span], pair_buf.at[span], pair_sem.at[g])
 
+    small = [
+        pltpu.make_async_copy(src, dst, small_sem.at[k])
+        for k, (src, dst) in enumerate(
+            [(slot_hbm, slot_ref), (len_hbm, len_ref), (block_hbm, block_ref), (occ_hbm, occ_ref),
+             (energy_hbm, energy_ref)]
+        )
+    ]
+    for k in (0, 1):
+        small[k].start()
     for g in range(groups):
         load(g).start()
+    for k in (2, 3, 4):
+        small[k].start()
     barrier = pltpu.get_barrier_semaphore()
     peers = [(2 * y + other, aux)]
     for d in range(1, ny):
@@ -231,7 +244,7 @@
         part = gram_ref.at[piece_of(lax.rem(x + nx - e, nx), lax.rem(z + nz - f, nz))]
         return copy(part, part, gx_ss.at[e, f], gx_rs.at[e, f], occ, z * nx + at_x(e))
 
-    half = domain // 2
+    half = domain // PIECES
 
     def row_copy(d, swap, h):
         target = 2 * at_y(d) + (other if swap else core)
@@ -270,7 +283,10 @@
                 place += 1
 
     early = [(d, 0, 0) for d in range(1, ny)]
-    late = [(d, 0, 1) for d in range(1, ny)] + [(d, 1, h) for d in far_y for h in (0, 1)]
+    late = [(d, 0, h) for d in range(1, ny) for h in range(1, PIECES)]
+    late += [(d, 1, h) for d in far_y for h in range(PIECES)]
+    for k in range(5):
+        small[k].wait()
     for g in range(groups):
         load(g).wait()
     for d in range(1, ny):
@@ -374,9 +390,9 @@
     nz = n_aux // nx
     piece = height // n_aux
     dma = pltpu.SemaphoreType.DMA
-    sems = [(ny, nx)] * 4 + [(nx, nz)] * 2 + [(nz,)] * 4 + [(nx, nz)] * 2 + [(ny, 2, 2)] * 2
+    sems = [(ny, nx)] * 4 + [(nx, nz)] * 2 + [(nz,)] * 4 + [(nx, nz)] * 2 + [(ny, 2, PIECES)] * 2
     sems += [(groups,), ()]
-    smem = pl.BlockSpec(memory_space=pltpu.SMEM)
+    hbm = pl.BlockSpec(memory_space=pltpu.HBM)
     vmem = pl.BlockSpec(memory_space=pltpu.VMEM)
     return pl.pallas_call(
         functools.partial(exchange_kernel, ny, nx, nz),
@@ -386,9 +402,15 @@
             jax.ShapeDtypeStruct((domain, domain), BF16),
             jax.ShapeDtypeStruct((8, lanes), F32),
         ),
-        in_specs=[smem] * 4 + [vmem, pl.BlockSpec(memory_space=pltpu.HBM)],
-        out_specs=[vmem] * 4,
+        in_specs=[hbm] * 6,
+        out_specs=[vmem, hbm, vmem, vmem],
         scratch_shapes=[
+            pltpu.SMEM(slot_orbital.shape, jnp.int32),
+            pltpu.SMEM(domain_len.shape, jnp.int32),
+            pltpu.SMEM(domain_blocks.shape, jnp.int32),
+            pltpu.SMEM(occ_energy.shape, F32),
+            pltpu.VMEM(table.shape, F32),
+            dma((5,)),
             pltpu.VMEM((domain, domain), BF16),
             pltpu.VMEM((domain, domain), BF16),
             pltpu.VMEM((domain, domain), F32),
@@ -405,19 +427,23 @@
             pltpu.VMEM((nz, piece, lanes), F32),
         ] + [dma(shape) for shape in sems],
         compiler_params=pltpu.CompilerParams(
-            collective_id=0, has_side_effects=True, vmem_limit_bytes=48 << 20
+            collective_id=0, has_side_effects=True, vmem_limit_bytes=60 << 20
         ),
         name="exchange",
     )(slot_orbital, domain_len, domain_blocks, occ_energy, table, pair_ints)
 
 
 def project_kernel(
-    slot_ref, len_ref, block_ref, occ_ref, packed_ref, own_ref, filter_ref, norm_ref, energy_hbm, out_hbm,
-    m_high, m_low, x_ref, r_ref, out_buf, energy_buf, out_sem, energy_sem,
+    slot_hbm, len_hbm, block_hbm, occ_hbm, packed_hbm, own_hbm, filter_ref, norm_ref, energy_hbm, out_hbm,
+    packed_ref, own_ref, own_sem, slot_ref, len_ref, block_ref, occ_ref, small_sem, m_high, m_low, x_ref, r_ref, out_buf, energy_buf, out_sem, energy_sem,
 ):
     tiles, _, width = out_buf.shape
     blocks, _, side = energy_buf.shape
-    orbital = slot_ref[lax.axis_index("occ")]
+    def fetch(t):
+        return pltpu.make_async_copy(own_hbm.at[t], own_ref.at[t], own_sem.at[t])
+
+    for t in range(tiles):
+        fetch(t).start()
     good = jnp.max(norm_ref[...]) < RESIDUAL_BOUND
 
     @pl.when(good)
@@ -426,6 +452,13 @@
 
     @pl.when(jnp.logical_not(good))
     def _():
+        small = [(slot_hbm, slot_ref), (len_hbm, len_ref), (block_hbm, block_ref), (occ_hbm, occ_ref), (packed_hbm, packed_ref)]
+        for k, (source, target) in enumerate(small):
+            move = pltpu.make_async_copy(source, target, small_sem.at[k])
+            move.start()
+            move.wait()
+        orbital = slot_ref[lax.axis_index("occ")]
+
         def energy(k):
             return pltpu.make_async_copy(
                 energy_hbm.at[block_ref[orbital, k]], energy_buf.at[k], energy_sem.at[k]
@@ -447,6 +480,7 @@
         )
 
     for t in range(tiles):
+        fetch(t).wait()
         out_buf[t] = dot(m_high[...], own_ref[t]).astype(BF16)
         flush(t).start()
     for t in range(tiles):
@@ -458,13 +492,21 @@
     blocks = domain_blocks.shape[1]
     side = size // blocks
     vmem = pl.BlockSpec(memory_space=pltpu.VMEM)
-    smem = pl.BlockSpec(memory_space=pltpu.SMEM)
+    hbm = pl.BlockSpec(memory_space=pltpu.HBM)
     return pl.pallas_call(
         project_kernel,
         out_shape=jax.ShapeDtypeStruct((size, groups * width), BF16),
-        in_specs=[smem] * 4 + [vmem] * 4 + [pl.BlockSpec(memory_space=pl.ANY)],
+        in_specs=[hbm] * 6 + [vmem] * 2 + [hbm],
         out_specs=pl.BlockSpec(memory_space=pl.ANY),
         scratch_shapes=[
+            pltpu.VMEM(packed.shape, F32),
+            pltpu.VMEM(own.shape, BF16),
+            pltpu.SemaphoreType.DMA((groups,)),
+            pltpu.SMEM(slot_orbital.shape, jnp.int32),
+            pltpu.SMEM(domain_len.shape, jnp.int32),
+            pltpu.SMEM(domain_blocks.shape, jnp.int32),
+            pltpu.SMEM(occ_energy.shape, F32),
+            pltpu.SemaphoreType.DMA((5,)),
             pltpu.VMEM((size, size), BF16),
             pltpu.VMEM((size, size), BF16),
             pltpu.VMEM((size, size), F32),
@@ -474,7 +516,7 @@
             pltpu.SemaphoreType.DMA((groups,)),
             pltpu.SemaphoreType.DMA((blocks,)),
         ],
-        compiler_params=pltpu.CompilerParams(vmem_limit_bytes=24 << 20),
+        compiler_params=pltpu.CompilerParams(vmem_limit_bytes=60 << 20),
         name="project",
     )(slot_orbital, domain_len, domain_blocks, occ_energy, packed, own, projector, norm, table)
 

time: 65.4 us -> 62.6 us (0.957)
  local copies, waits for them, and re-layouts: 3.63 us -> 0 us
  Pallas kernels: 61.5 us -> 62.4 us
    unnamed x10 -> x0, local copies, waits for them, and re-layouts: 3.63 us -> none
    pallas_call x1, Pallas kernels: 3.49 us -> 5.92 us  [project(): pl.pallas_call(project_kernel, out_shape=jax.ShapeDtypeStruct((size, grou...]
    pallas_call x1, Pallas kernels: 58 us -> 56.5 us  [exchange(): pl.pallas_call(functools.partial(exchange_kernel, ny, nx, nz), out_shape=...]
where the time goes in v5:
time: 62.6 us; the launch traced here: 62.4 us
  Pallas kernels  62.4 us (100%)
    pallas_call x1, Pallas kernels, exchange(): pl.pallas_call(functools.partial(exchange_kernel, ny, nx, nz), out_shape=...  56.5 us
    pallas_call x1, Pallas kernels, project(): pl.pallas_call(project_kernel, out_shape=jax.ShapeDtypeStruct((size, grou...  5.92 us

profile of v5, /device:TPU:0, one launch (start us, length us, event | category | flops | bytes accessed | tf_op | source)
XLA Modules:
  0.0 62.4 jit_solution(18037585986301212552)
XLA Ops:
  0.0 56.5 %exchange.1 = (f32[1280,128]{1,0:T(8,128)}, bf16[4,512,640]{2,1,0:T(8,128)(2,1)}, bf16[512,512]{1,0:T(8,128)(2,1)}, f32[8,128]{1,0:T(8,128)}) custom-call(s32[4]{0:T(128)} %slot_hbm.3, s32[4]{0:T(128)} %len_hbm.3, s32[4,4]{1,0:T(4,128)} %block_hbm.3, f32[4]{0:T(128)} %occ_hbm.3, f32[704,1,128]{2,1,0:T(1,128)} %bitcast.2, bf16[16,128,640]{2,1,0:T(8,128)(2,1)} %pair_hbm.1), custom_call_target="tpu_custom_call" | custom-call | tf_op jit(solution)/shard_map/exchange/pallas_call | solution.py:397
  56.5 5.9 %project.1 = bf16[512,2560]{1,0:T(8,128)(2,1)} custom-call(s32[4]{0:T(128)} %slot_hbm.3, s32[4]{0:T(128)} %len_hbm.3, s32[4,4]{1,0:T(4,128)} %block_hbm.3, f32[4]{0:T(128)} %occ_hbm.3, f32[1280,128]{1,0:T(8,128)} %get-tuple-element.9.packed_hbm, bf16[4,512,640]{2,1,0:T(8,128)(2,1)} %get-tuple-element.10.own_hbm, ...), custom_call_target="tpu_custom_call" | custom-call | tf_op jit(solution)/shard_map/project/pallas_call | solution.py:496
